TPU v7x, 128 devices: a whole 4x4x4 slice. The times are simulated.
128 devices in a mesh: dp: 2 (over core), ctx: 16 (over z, y), head: 4 (over x).
Axes of the slice: x: 4, y: 4, z: 4, core: 2. Of those that a mesh axis runs over, the one named last changes fastest.
Arguments:
- queries: float32 [2, 4096, 64, 128], P('dp', 'ctx', 'head'), may hold values from -8 to 8
- key_rows: float32 [2, 4096, 8, 128], P('dp', 'ctx', 'head'), may hold values from -8 to 8
- value_rows: float32 [2, 4096, 8, 128], P('dp', 'ctx', 'head'), may hold values from -18 to 18
- query_map: float32 [64, 128, 128], P('head'), may hold values from -0.5 to 0.5
- key_map: float32 [8, 128, 128], P('head'), may hold values from -0.5 to 0.5
- block_doc: int32 [2, 16], P('dp'), may hold values from 0 to 4, never falling along the last dimension, each value on 1 to 9 neighbouring positions
Outputs:
- grad_queries: float32 [2, 4096, 64, 128], P('dp', 'ctx', 'head')
- grad_keys: float32 [2, 4096, 8, 128], P('dp', 'ctx', 'head')
- grad_values: float32 [2, 4096, 8, 128], P('dp', 'ctx', 'head')
- grad_query_map: float32 [64, 128, 128], P('head')
- grad_key_map: float32 [8, 128, 128], P('head')
Inputs may be any that keep to these rules, and one draw needn't show every extreme that they name: `block_doc`: the document numbers of a sequence's blocks never fall along the sequence; each document covers 1 to 9 blocks in a row, and some document covers exactly 9.
All inputs are finite; a program needn't handle non-finite values.
Results may differ from a plain program's by a relative error of at most 0.0003.
Values sent between devices are 32-bit elements; how exact they have to be, the bound alone decides.
No kernel may reach another device: no remote copies, remote signals or barrier semaphores. Data moves between devices by JAX's collectives and lax.ppermute only.
A program may use at most 128 MiB of HBM per device.

v0:
```python
import math

import jax
import jax.numpy as jnp
from jax import lax
from jax.experimental import pallas as pl
from jax.experimental.pallas import tpu as pltpu
from jax.sharding import Mesh
from jax.sharding import PartitionSpec as P

CTX = ("ctx_0", "ctx_1")
DP_CTX = ("dp", "ctx_0", "ctx_1")
F32 = jnp.float32
BF16 = jnp.bfloat16
LOG2E = 1.0 / math.log(2.0)
TOK = 256
WID = 128
GRP = 8
KVH = 2
HEADS = GRP * KVH
STEP = 2
N_CTX = 16
SROWS = WID + 8


def split(x):
    hi = x.astype(BF16)
    return hi, (x - hi.astype(F32)).astype(BF16)


def dot(a, b, ca, cb):
    return lax.dot_general(a, b, (((ca,), (cb,)), ((), ())), preferred_element_type=F32)


def deep(a, b, ca, cb):
    ah, al = a
    bh, bl = b
    return dot(jnp.concatenate([ah, al], ca), jnp.concatenate([bh, bh], cb), ca, cb) + dot(ah, bl, ca, cb)


def wide(a, b, ca, cb):
    ah, al = a
    bh, bl = b
    n = bh.shape[1 - cb]
    both = dot(ah, jnp.concatenate([bh, bl], 1 - cb), ca, cb)
    return both[:, :n] + both[:, n:] + dot(al, bh, ca, cb)


def softmax(x):
    e = jnp.exp(x - jnp.max(x, axis=-1, keepdims=True))
    return e / jnp.sum(e, axis=-1, keepdims=True)


def local_kernel(q_ref, k_ref, v_ref, w_ref, wk_ref, qf_ref, num_ref, acc_ref, stat_ref, a_ref, kf_ref):
    @pl.when(pl.program_id(0) % (GRP // STEP) == 0)
    def _():
        kf_ref[0] = softmax(deep(split(k_ref[0]), split(wk_ref[0]), 1, 0))

    k, v, kf = split(k_ref[0]), split(v_ref[0]), split(kf_ref[0])
    causal = lax.broadcasted_iota(jnp.int32, (TOK, TOK), 0) >= lax.broadcasted_iota(jnp.int32, (TOK, TOK), 1)
    lane = lax.broadcasted_iota(jnp.int32, (TOK, WID), 1)
    for i in range(STEP):
        q = q_ref[i]
        qf = softmax(deep(split(q), split(w_ref[i]), 1, 0))
        qf_ref[i] = qf
        a = jnp.where(causal, deep(split(qf), kf, 1, 1), 0.0)
        a_ref[i] = a
        num_ref[i] = wide(split(a), v, 1, 0)
        den = jnp.sum(a, axis=-1, keepdims=True)
        s = deep(split(q * (LOG2E / math.sqrt(WID))), k, 1, 1)
        s = jnp.where(causal, s, -1e30)
        m = jnp.max(s, axis=-1, keepdims=True)
        p = jnp.where(causal, jnp.exp2(s - m), 0.0)
        acc_ref[i] = wide(split(p), v, 1, 0)
        l = jnp.sum(p, axis=-1, keepdims=True)
        stat_ref[i] = jnp.where(lane == 0, m, jnp.where(lane == 1, l, den))


def teacher_kernel(pos, q_ref, acc0_ref, stat_ref, kv_ref, wk_ref, t_ref, sq_ref, p_ref, n_ref, buf, sem, qs, m_sc, l_sc, acc):
    first, own = pos[0], pos[1]
    rows = STEP * TOK
    tiles = GRP // STEP

    def fetch(j, slot):
        return pltpu.make_async_copy(kv_ref.at[j], buf.at[slot], sem.at[slot])

    @pl.when(first < own)
    def _():
        fetch(first, 0).start()

    lane = lax.broadcasted_iota(jnp.int32, (rows, WID), 1)
    for i in range(tiles):
        here = pl.ds(i * rows, rows)
        q = q_ref[i * STEP : (i + 1) * STEP].reshape(rows, WID) * (LOG2E / math.sqrt(WID))
        hi, lo = split(q)
        qs[here, :WID] = hi
        qs[here, WID:] = lo
        stat = stat_ref[i * STEP : (i + 1) * STEP].reshape(rows, WID)
        m_sc[here, :] = jnp.broadcast_to(stat[:, 0:1], (rows, WID))
        l_sc[here, :] = jnp.where(lane == 1, stat, 0.0)
        acc[here, :] = acc0_ref[i * STEP : (i + 1) * STEP].reshape(rows, WID)
    p_ref[...] = jnp.zeros_like(p_ref)
    n_ref[...] = jnp.zeros_like(n_ref)
    wk = split(wk_ref[0])

    def visit(j, carry):
        slot = lax.rem(j - first, 2)
        fetch(j, slot).wait()

        @pl.when(j + 1 < own)
        def _():
            fetch(j + 1, 1 - slot).start()

        kh, kl = split(buf[slot, 0])
        vh, vl = split(buf[slot, 1])
        k_twice = jnp.concatenate([kh, kh], 1)
        v_both = jnp.concatenate([vh, vl], 1)
        kf = softmax(deep((kh, kl), wk, 1, 0))
        p_ref[...] += wide(split(kf), (vh, vl), 0, 0)
        n_ref[...] += jnp.broadcast_to(jnp.sum(kf, axis=0, keepdims=True), n_ref.shape)
        for i in range(tiles):
            here = pl.ds(i * rows, rows)
            q = qs[here, :]
            s = dot(q, k_twice, 1, 1) + dot(q[:, :WID], kl, 1, 1)
            m_old = m_sc[here, :]
            m_new = jnp.maximum(m_old, jnp.max(s, axis=-1, keepdims=True))
            p = jnp.exp2(s - jnp.concatenate([m_new, m_new], 1))
            fade = jnp.exp2(m_old - m_new)
            m_sc[here, :] = m_new
            l_sc[here, :] = fade * l_sc[here, :] + p[:, :WID] + p[:, WID:]
            ph, pl_ = split(p)
            both = dot(ph, v_both, 1, 0)
            acc[here, :] = fade * acc[here, :] + both[:, :WID] + both[:, WID:] + dot(pl_, vh, 1, 0)
        return carry

    lax.fori_loop(first, own, visit, 0)
    total = jnp.zeros((TOK, WID), F32)
    for i in range(tiles):
        here = pl.ds(i * rows, rows)
        t = acc[here, :] / jnp.sum(l_sc[here, :], axis=-1, keepdims=True)
        t_ref[i * STEP : (i + 1) * STEP] = t.reshape(STEP, TOK, WID)
        for k in range(STEP):
            part = t[k * TOK : (k + 1) * TOK]
            total = total + part * part
    line = jnp.sum(total, axis=-1, keepdims=True)
    sq_ref[...] = jnp.transpose(jnp.broadcast_to(line, (TOK, WID)))[:8]


def student_kernel(
    pos, q_ref, qf_ref, num_ref, stat_ref, a_ref, t0_ref, t1_ref, w_ref, k_ref, v_ref, kf_ref, p0_ref, p1_ref,
    n0_ref, n1_ref, sq0_ref, sq1_ref, sq2_ref, sq3_ref, wk_ref, kv0_ref, kv1_ref,
    gq_ref, mq_ref, gkf_ref, gv_ref, s_ref, mk_ref, buf, sem,
):
    step = pl.program_id(0)
    per = GRP // STEP
    head = step // per
    first, own = pos[0], pos[1]

    @pl.when(step % per == 0)
    def _():
        gkf_ref[...] = jnp.zeros_like(gkf_ref)
        gv_ref[...] = jnp.zeros_like(gv_ref)
        s_ref[...] = jnp.zeros_like(s_ref)

    low = head == 0
    prior = split(jnp.where(low, p0_ref[...], p1_ref[...]))
    prior_n = jnp.where(low, n0_ref[...], n1_ref[...])[:1]
    v, kf = split(v_ref[0]), split(kf_ref[0])
    squares = sq0_ref[...] + sq1_ref[...] + sq2_ref[...] + sq3_ref[...]
    mean = squares / (4 * HEADS * WID) + 1e-6
    scale = jnp.transpose(2.0 / mean)[:, 0:1]
    causal = lax.broadcasted_iota(jnp.int32, (TOK, TOK), 0) >= lax.broadcasted_iota(jnp.int32, (TOK, TOK), 1)
    for i in range(STEP):
        qf = qf_ref[i]
        qfs = split(qf)
        teacher = jnp.where(low, t0_ref[i], t1_ref[i])
        num = num_ref[i] + deep(qfs, prior, 1, 0)
        den = stat_ref[i][:, 2:3] + jnp.sum(qf * prior_n, axis=-1, keepdims=True)
        inv = 1.0 / den
        student = num * inv
        gn = (student - teacher) * (scale * inv)
        gd = -jnp.sum(gn * student, axis=-1, keepdims=True)
        gns = split(gn)
        gs = jnp.where(causal, deep(gns, v, 1, 1) + gd, 0.0)
        gss = split(gs)
        gqf = deep(gns, prior, 1, 1) + gd * prior_n + wide(gss, kf, 1, 0)
        qlg = qf * (gqf - jnp.sum(qf * gqf, axis=-1, keepdims=True))
        qlgs = split(qlg)
        gq_ref[i] = deep(qlgs, split(w_ref[i]), 1, 1)
        mq_ref[i] = wide(split(q_ref[i]), qlgs, 0, 0)
        gkf_ref[0] += wide(gss, qfs, 0, 0)
        gv_ref[0] += wide(split(a_ref[i]), gns, 0, 0)
        s_ref[0, :WID] += wide(qfs, gns, 0, 0)
        s_ref[0, WID:] += jnp.broadcast_to(jnp.sum(qf * gd, axis=0, keepdims=True), (8, WID))

    def key_map_part(kv_ref):
        state = split(s_ref[0, :WID])
        norm = s_ref[0, WID : WID + 1]
        wk = split(wk_ref[0])

        def fetch(j, slot):
            return pltpu.make_async_copy(kv_ref.at[j], buf.at[slot], sem.at[slot])

        @pl.when(first < own)
        def _():
            fetch(first, 0).start()

        def logit_grad(feats, grad):
            return feats * (grad - jnp.sum(feats * grad, axis=-1, keepdims=True))

        mk_ref[0] = wide(split(k_ref[0]), split(logit_grad(kf_ref[0], gkf_ref[0])), 0, 0)

        def visit(j, carry):
            slot = lax.rem(j - first, 2)
            fetch(j, slot).wait()

            @pl.when(j + 1 < own)
            def _():
                fetch(j + 1, 1 - slot).start()

            ks = split(buf[slot, 0])
            feats = softmax(deep(ks, wk, 1, 0))
            grad = deep(split(buf[slot, 1]), state, 1, 1) + norm
            mk_ref[0] += wide(ks, split(logit_grad(feats, grad)), 0, 0)
            return carry

        lax.fori_loop(first, own, visit, 0)

    @pl.when(step == per - 1)
    def _():
        key_map_part(kv0_ref)

    @pl.when(step == 2 * per - 1)
    def _():
        key_map_part(kv1_ref)


def later_kernel(pos, s_ref, gkf_ref, gv_ref, kf_ref, v_ref, wk_ref, gk_ref, out_ref):
    own, last = pos[1], pos[2]
    for h in range(KVH):
        total = lax.fori_loop(
            own + 1, last + 1, lambda j, held: held + s_ref[j, h], jnp.zeros((SROWS, WID), F32)
        )
        state, norm = split(total[:WID]), total[WID : WID + 1]
        kf = kf_ref[h]
        gkf = gkf_ref[h] + deep(split(v_ref[h]), state, 1, 1) + norm
        out_ref[h] = gv_ref[h] + deep(split(kf), state, 1, 0)
        klg = kf * (gkf - jnp.sum(kf * gkf, axis=-1, keepdims=True))
        gk_ref[h] = deep(split(klg), split(wk_ref[h]), 1, 1)


def shape(*dims):
    return jax.ShapeDtypeStruct(dims, F32)


def full(*dims):
    return pl.BlockSpec(dims, lambda *_: (0,) * len(dims))


def params(limit=56):
    return pltpu.CompilerParams(vmem_limit_bytes=limit * 1024 * 1024)


def body(queries, key_rows, value_rows, query_map, key_map, block_doc):
    keys = jnp.transpose(key_rows[0], (1, 0, 2))
    values = jnp.transpose(value_rows[0], (1, 0, 2))
    gathered = []
    for h in range(KVH):
        pair = jnp.stack([keys[h], values[h]])
        gathered.append(lax.all_gather(pair, CTX))

    own = lax.axis_index(CTX).astype(jnp.int32)
    doc_table = block_doc[0]
    places = jnp.arange(N_CTX, dtype=jnp.int32)
    own_doc = jnp.sum(jnp.where(places == own, doc_table, 0))
    first = jnp.sum((doc_table < own_doc).astype(jnp.int32))
    last = jnp.sum((doc_table <= own_doc).astype(jnp.int32)) - 1
    pos = jnp.stack([first, own, last])

    q = jnp.transpose(queries[0], (1, 0, 2))
    per = GRP // STEP
    by_head = lambda *dims: pl.BlockSpec((STEP, *dims), lambda g, *_: (g, 0, 0))
    by_kv = lambda *dims: pl.BlockSpec((1, *dims), lambda g, *_: (g // per, 0, 0))
    qf, num, acc0, stat, a, kf = pl.pallas_call(
        local_kernel,
        grid=(HEADS // STEP,),
        in_specs=[by_head(TOK, WID), by_kv(TOK, WID), by_kv(TOK, WID), by_head(WID, WID), by_kv(WID, WID)],
        out_specs=[by_head(TOK, WID)] * 4 + [by_head(TOK, TOK), by_kv(TOK, WID)],
        out_shape=[shape(HEADS, TOK, WID)] * 4 + [shape(HEADS, TOK, TOK), shape(KVH, TOK, WID)],
        compiler_params=params(),
        name="local",
    )(q, keys, values, query_map, key_map)

    any_spec = pl.BlockSpec(memory_space=pl.ANY)
    parts = []
    for h in range(KVH):
        of = lambda *dims, h=h: pl.BlockSpec((GRP, *dims), lambda g, *_: (h, 0, 0))
        parts.append(
            pl.pallas_call(
                teacher_kernel,
                grid_spec=pltpu.PrefetchScalarGridSpec(
                    num_scalar_prefetch=1,
                    grid=(1,),
                    in_specs=[
                        of(TOK, WID),
                        of(TOK, WID),
                        of(TOK, WID),
                        any_spec,
                        pl.BlockSpec((1, WID, WID), lambda g, *_, h=h: (h, 0, 0)),
                    ],
                    out_specs=[full(GRP, TOK, WID), full(8, TOK), full(WID, WID), full(8, WID)],
                    scratch_shapes=[
                        pltpu.VMEM((2, 2, TOK, WID), F32),
                        pltpu.SemaphoreType.DMA((2,)),
                        pltpu.VMEM((GRP * TOK, 2 * WID), BF16),
                        pltpu.VMEM((GRP * TOK, WID), F32),
                        pltpu.VMEM((GRP * TOK, WID), F32),
                        pltpu.VMEM((GRP * TOK, WID), F32),
                    ],
                ),
                out_shape=[shape(GRP, TOK, WID), shape(8, TOK), shape(WID, WID), shape(8, WID)],
                compiler_params=params(),
                name="teacher",
            )(pos, q, acc0, stat, gathered[h], key_map)
        )
    (t0, sq_a, p0, n0), (t1, sq_b, p1, n1) = parts
    squares = sq_a + sq_b
    others = [lax.ppermute(squares, "head", [(i, (i + k) % 4) for i in range(4)]) for k in (1, 2, 3)]

    half = lambda c: pl.BlockSpec(
        (STEP, TOK, WID), lambda g, *_: ((jnp.minimum(g, per - 1) if c == 0 else jnp.maximum(g - per, 0)), 0, 0)
    )
    gq, mq, gkf, gv, states, mk = pl.pallas_call(
        student_kernel,
        grid_spec=pltpu.PrefetchScalarGridSpec(
            num_scalar_prefetch=1,
            grid=(HEADS // STEP,),
            in_specs=[
                by_head(TOK, WID), by_head(TOK, WID), by_head(TOK, WID), by_head(TOK, WID), by_head(TOK, TOK),
                half(0), half(1), by_head(WID, WID), by_kv(TOK, WID), by_kv(TOK, WID), by_kv(TOK, WID),
                full(WID, WID), full(WID, WID), full(8, WID), full(8, WID),
                full(8, TOK), full(8, TOK), full(8, TOK), full(8, TOK),
                by_kv(WID, WID), any_spec, any_spec,
            ],
            out_specs=[
                by_head(TOK, WID), by_head(WID, WID), by_kv(TOK, WID), by_kv(TOK, WID), by_kv(SROWS, WID),
                by_kv(WID, WID),
            ],
            scratch_shapes=[pltpu.VMEM((2, 2, TOK, WID), F32), pltpu.SemaphoreType.DMA((2,))],
        ),
        out_shape=[
            shape(HEADS, TOK, WID), shape(HEADS, WID, WID), shape(KVH, TOK, WID), shape(KVH, TOK, WID),
            shape(KVH, SROWS, WID), shape(KVH, WID, WID),
        ],
        compiler_params=params(),
        name="student",
    )(pos, q, qf, num, stat, a, t0, t1, query_map, keys, values, kf, p0, p1, n0, n1,
      squares, *others, key_map, *gathered)

    all_states = lax.all_gather(states, CTX)
    maps = jnp.concatenate([mq, mk]).reshape(32, -1, WID)
    maps = jnp.sum(lax.all_to_all(maps, DP_CTX, 0, 0, tiled=True), axis=0)
    maps = lax.all_to_all(jnp.broadcast_to(maps, (32, *maps.shape)), DP_CTX, 0, 0, tiled=True)
    maps = maps.reshape(HEADS + KVH, WID, WID)

    grad_keys, grad_values = pl.pallas_call(
        later_kernel,
        grid_spec=pltpu.PrefetchScalarGridSpec(
            num_scalar_prefetch=1,
            grid=(1,),
            in_specs=[full(N_CTX, KVH, SROWS, WID)] + [full(KVH, TOK, WID)] * 4 + [full(KVH, WID, WID)],
            out_specs=[full(KVH, TOK, WID)] * 2,
        ),
        out_shape=[shape(KVH, TOK, WID)] * 2,
        compiler_params=params(),
        name="later",
    )(pos, all_states, gkf, gv, kf, values, key_map)
    back = lambda x: jnp.transpose(x, (1, 0, 2))[None]
    return (back(gq), back(grad_keys), back(grad_values), maps[:HEADS], maps[HEADS:])


def solution(mesh):
    torus = Mesh(
        mesh.devices.reshape(mesh.shape["dp"], 4, 4, mesh.shape["head"]),
        ("dp", "ctx_0", "ctx_1", "head"),
    )
    rows = P("dp", CTX, "head", None)
    placed = (rows, rows, rows, P("head", None, None), P("head", None, None), P("dp", None))
    return jax.shard_map(
        body, mesh=torus, in_specs=placed, out_specs=(rows, rows, rows, placed[3], placed[4]), check_vma=False
    )
```

profile of v0, /device:TPU:1, one launch (start us, length us, event | category | flops | bytes accessed | tf_op | source)
XLA Modules:
  0.0 261.7 jit_solution(180323437860474600)
XLA Ops:
  7.2 0.0 copy-start.2
  7.2 0.0 all-gather.9.cloned.1.call-start
  7.2 1.2 copy_bitcast_fusion.1
  8.4 0.0 copy-start
  8.4 0.0 copy-start.1
  8.5 0.8 pad_maximum_fusion.2
  9.3 0.0 all-gather.9.cloned.1.call-update
  9.3 0.0 all-gather.7.cloned.1.call-start
  9.4 0.7 pad_maximum_fusion.1
  10.1 0.0 all-gather.7.cloned.1.call-update
  10.1 0.0 all-gather.11.cloned.1.call-start
  10.2 0.0 copy-done.2
  10.2 0.0 copy-start.9
  10.2 2.0 copy.26
  12.2 0.0 copy-done
  12.2 0.0 copy-done.1
  12.2 0.7 fusion
  12.8 1.3 fusion.1
  14.8 16.5 %local.1 = (f32[16,256,128]{2,1,0:T(8,128)}, f32[16,256,128]{2,1,0:T(8,128)}, f32[16,256,128]{2,1,0:T(8,128)}, f32[16,256,128]{2,1,0:T(8,128)}, f32[16,256,256]{2,1,0:T(8,128)}, /*index=5*/f32[2,256,128]{2,1,0:T(8,128)}) custom-call(f32[16,256,128]{2,1,0:T(8,128)} %bitcast.34, f32[2,256,128]{2,1,0:T(8,128)} %copy-done.1, f32[2,256,128]{2,1,0:T(8,128)} %copy-done, ...), custom_call_target="tpu_custom_call" | custom-call | tf_op jit(solution)/shard_map/local/pallas_call | solution.py:284
  31.3 1.3 pad_add_fusion.pos
  32.6 32.1 %all-gather.9.cloned.1.call-done = f32[32,256,128]{2,1,0:T(8,128)} async-done(((f32[2,256,128]{2,1,0:T(8,128)}), f32[32,256,128]{2,1,0:T(8,128)}) %all-gather.9.cloned.1.call-update) | async-done | bytes 4194320 | tf_op jit(solution)/shard_map/all_gather | solution.py:270
  64.7 4.6 %teacher.3 = (f32[8,256,128]{2,1,0:T(8,128)}, f32[8,256]{1,0:T(8,128)}, f32[128,128]{1,0:T(8,128)}, f32[8,128]{1,0:T(8,128)}) custom-call(s32[3]{0:T(128)} %pad_add_fusion.pos, f32[16,256,128]{2,1,0:T(8,128)} %bitcast.35, f32[16,256,128]{2,1,0:T(8,128)} %get-tuple-element.31.acc0_ref, f32[16,256,128]{2,1,0:T(8,128)} %get-tuple-element.29.stat_ref, ...), custom_call_target="tpu_custom_call" | custom-call | tf_op jit(solution)/shard_map/teacher/pallas_call | solution.py:299
  69.3 49.2 %all-gather.7.cloned.1.call-done = f32[32,256,128]{2,1,0:T(8,128)} async-done(((f32[2,256,128]{2,1,0:T(8,128)}), f32[32,256,128]{2,1,0:T(8,128)}) %all-gather.7.cloned.1.call-update) | async-done | bytes 4194320 | tf_op jit(solution)/shard_map/all_gather | solution.py:270
  118.6 4.7 %teacher.2 = (f32[8,256,128]{2,1,0:T(8,128)}, f32[8,256]{1,0:T(8,128)}, f32[128,128]{1,0:T(8,128)}, f32[8,128]{1,0:T(8,128)}) custom-call(s32[3]{0:T(128)} %pad_add_fusion.pos, f32[16,256,128]{2,1,0:T(8,128)} %bitcast.36, f32[16,256,128]{2,1,0:T(8,128)} %get-tuple-element.31.acc0_ref, f32[16,256,128]{2,1,0:T(8,128)} %get-tuple-element.29.stat_ref, ...), custom_call_target="tpu_custom_call" | custom-call | tf_op jit(solution)/shard_map/teacher/pallas_call | solution.py:299
  123.3 0.7 add.8.sq0_ref
  124.0 2.4 collective-permute-start.2
  126.4 0.6 collective-permute-start.1
  127.0 0.6 collective-permute-start
  127.6 0.0 collective-permute-done.2.sq3_ref
  127.6 2.9 %collective-permute-done.1.sq2_ref = f32[8,256]{1,0:T(8,128)S(1)} collective-permute-done((f32[8,256]{1,0:T(8,128)S(1)}, f32[8,256]{1,0:T(8,128)S(1)}, u32[]{:S(2)}, u32[]{:S(2)}) %collective-permute-start.1) | collective-permute-done | bytes 8224 | tf_op jit(solution)/shard_map/ppermute | solution.py:328
  130.4 0.3 collective-permute-done.sq1_ref
  130.7 0.3 copy-done.6
  131.0 0.3 copy-done.7
  131.3 24.1 %student.1 = (f32[16,256,128]{2,1,0:T(8,128)}, f32[16,128,128]{2,1,0:T(8,128)}, f32[2,256,128]{2,1,0:T(8,128)}, f32[2,256,128]{2,1,0:T(8,128)}, f32[2,136,128]{2,1,0:T(8,128)}, /*index=5*/f32[2,128,128]{2,1,0:T(8,128)}) custom-call(s32[3]{0:T(128)} %pad_add_fusion.pos, f32[16,256,128]{2,1,0:T(8,128)} %bitcast.37, f32[16,256,128]{2,1,0:T(8,128)} %get-tuple-element.27.qf_ref, ...), custom_call_target="tpu_custom_call" | custom-call | tf_op jit(solution)/shard_map/student/pallas_call | solution.py:333
  155.4 0.0 all-gather.11.cloned.1.call-update
  155.4 1.4 pad_maximum_fusion
  156.8 57.9 %all_to_all.10 = f32[32,72,128]{2,1,0:T(8,128)S(1)} all-to-all(f32[32,72,128]{2,1,0:T(8,128)S(1)} %bitcast.44), channel_id=1, replica_groups=mesh['dp'=2,'ctx_0'=4,'ctx_1'=4,'head'=4] {'dp','ctx_0','ctx_1'}, dimensions={0} | all-to-all | bytes 2359296 | tf_op jit(solution)/shard_map/all_to_all | solution.py:362
  214.8 0.1 reduce_sum.39
  214.8 1.1 broadcast_in_dim.20
  215.9 4.2 %all-to-all-start.1 = ((f32[32,72,128]{2,1,0:T(8,128)}), f32[32,72,128]{2,1,0:T(8,128)S(1)}, u32[]{:S(2)}, u32[]{:S(2)}) async-start(f32[32,72,128]{2,1,0:T(8,128)} %broadcast_in_dim.20), calls=%async_computation.1 | async-start | bytes 2359296 | tf_op jit(solution)/shard_map/all_to_all | solution.py:363
  220.2 0.0 copy-done.3
  220.2 2.5 copy.20
  222.7 22.8 %all-to-all-done.1 = f32[32,72,128]{2,1,0:T(8,128)S(1)} async-done(((f32[32,72,128]{2,1,0:T(8,128)}), f32[32,72,128]{2,1,0:T(8,128)S(1)}, u32[]{:S(2)}, u32[]{:S(2)}) %all-to-all-start.1) | async-done | bytes 1179680 | tf_op jit(solution)/shard_map/all_to_all | solution.py:363
  245.5 0.7 slice.29
  246.1 1.0 slice.28
  247.2 4.3 %later.1 = (f32[2,256,128]{2,1,0:T(8,128)}, f32[2,256,128]{2,1,0:T(8,128)}) custom-call(s32[3]{0:T(128)} %pad_add_fusion.pos, f32[16,2,136,128]{3,2,1,0:T(8,128)} %bitcast.45, f32[2,256,128]{2,1,0:T(8,128)} %get-tuple-element.43.gkf_ref, f32[2,256,128]{2,1,0:T(8,128)} %get-tuple-element.44.gv_ref, f32[2,256,128]{2,1,0:T(8,128)} %get-tuple-element.34.kf_ref, ...), custom_call_target="tpu_custom_call" | custom-call | tf_op jit(solution)/shard_map/later/pallas_call | solution.py:366
  251.5 1.9 copy.21
  253.4 1.9 copy.22
  (13 shorter events, 0.1 us)
Async XLA Ops:
  7.2 3.0 %copy-start.2 = (f32[1,256,16,128]{3,2,1,0:T(8,128)S(1)}, f32[1,256,16,128]{3,2,1,0:T(8,128)}, u32[]{:S(2)}) copy-start(f32[1,256,16,128]{3,2,1,0:T(8,128)} %param.6) | copy-start | bytes 6291460
  7.2 57.5 %all-gather.9.cloned.1.call-start = ((), (), s32[]{:S(2)}) async-start(), calls=%async_computation.3 | async-start | bytes 4456448 | tf_op jit(solution)/shard_map/all_gather | solution.py:270
  8.4 3.7 %copy-start = (f32[2,256,128]{2,1,0:T(8,128)}, f32[2,256,128]{2,1,0:T(8,128)S(1)}, u32[]{:S(2)}) copy-start(f32[2,256,128]{2,1,0:T(8,128)S(1)} %get-tuple-element.65.v_ref) | copy-start | bytes 786436
  8.4 3.7 %copy-start.1 = (f32[2,256,128]{2,1,0:T(8,128)}, f32[2,256,128]{2,1,0:T(8,128)S(1)}, u32[]{:S(2)}) copy-start(f32[2,256,128]{2,1,0:T(8,128)S(1)} %get-tuple-element.66.k_ref) | copy-start | bytes 786436
  9.3 109.2 %all-gather.7.cloned.1.call-start = ((), (), s32[]{:S(2)}) async-start(), calls=%async_computation.2 | async-start | bytes 4456448 | tf_op jit(solution)/shard_map/all_gather | solution.py:270
  10.1 237.1 %all-gather.11.cloned.1.call-start = ((), (), s32[]{:S(2)}) async-start(), calls=%async_computation.4 | async-start | bytes 2367488 | tf_op jit(solution)/shard_map/all_gather | solution.py:360
  10.2 2.0 copy-start.9
  118.6 4.7 %copy-start.8 = (f32[8,256]{1,0:T(8,128)S(1)}, f32[8,256]{1,0:T(8,128)}, u32[]{:S(2)}) copy-start(f32[8,256]{1,0:T(8,128)} %get-tuple-element.40) | copy-start | bytes 24580
  124.0 6.7 %copy-start.4 = (f32[8,256]{1,0:T(8,128)}, f32[8,256]{1,0:T(8,128)S(1)}, u32[]{:S(2)}) copy-start(f32[8,256]{1,0:T(8,128)S(1)} %add.8.sq0_ref) | copy-start | bytes 24580
  124.0 3.6 %collective-permute-start.2 = (f32[8,256]{1,0:T(8,128)S(1)}, f32[8,256]{1,0:T(8,128)S(1)}, u32[]{:S(2)}, u32[]{:S(2)}) collective-permute-start(f32[8,256]{1,0:T(8,128)S(1)} %add.8.sq0_ref), channel_id=1, source_target_pairs={{0,3},{1,0},{2,1},{3,2},{4,7},{5,4},{6,5},{7,6},{8,11},{9,8},{10,9... | collective-permute-start | bytes 24584 | tf_op jit(solution)/shard_map/ppermute | solution.py:328
  126.4 4.0 %collective-permute-start.1 = (f32[8,256]{1,0:T(8,128)S(1)}, f32[8,256]{1,0:T(8,128)S(1)}, u32[]{:S(2)}, u32[]{:S(2)}) collective-permute-start(f32[8,256]{1,0:T(8,128)S(1)} %add.8.sq0_ref), channel_id=1, source_target_pairs={{0,2},{1,3},{2,0},{3,1},{4,6},{5,7},{6,4},{7,5},{8,10},{9,11},{10,... | collective-permute-start | bytes 24584 | tf_op jit(solution)/shard_map/ppermute | solution.py:328
  127.0 3.7 %collective-permute-start = (f32[8,256]{1,0:T(8,128)S(1)}, f32[8,256]{1,0:T(8,128)S(1)}, u32[]{:S(2)}, u32[]{:S(2)}) collective-permute-start(f32[8,256]{1,0:T(8,128)S(1)} %add.8.sq0_ref), channel_id=1, source_target_pairs={{0,1},{1,2},{2,3},{3,0},{4,5},{5,6},{6,7},{7,4},{8,9},{9,10},{10,1... | collective-permute-start | bytes 24584 | tf_op jit(solution)/shard_map/ppermute | solution.py:328
  127.6 3.1 %copy-start.5 = (f32[8,256]{1,0:T(8,128)}, f32[8,256]{1,0:T(8,128)S(1)}, u32[]{:S(2)}) copy-start(f32[8,256]{1,0:T(8,128)S(1)} %collective-permute-done.2.sq3_ref) | copy-start | bytes 24580
  130.4 0.6 copy-start.6
  130.7 0.6 copy-start.7
  214.8 5.4 %copy-start.3 = (f32[16,256,128]{2,1,0:T(8,128)S(1)}, f32[16,256,128]{2,1,0:T(8,128)}, u32[]{:S(2)}) copy-start(f32[16,256,128]{2,1,0:T(8,128)} %get-tuple-element.41) | copy-start | bytes 6291460
  215.9 29.5 %all-to-all-start.1 = ((f32[32,72,128]{2,1,0:T(8,128)}), f32[32,72,128]{2,1,0:T(8,128)S(1)}, u32[]{:S(2)}, u32[]{:S(2)}) async-start(f32[32,72,128]{2,1,0:T(8,128)} %broadcast_in_dim.20), calls=%async_computation.1 | async-start | bytes 2359296 | tf_op jit(solution)/shard_map/all_to_all | solution.py:363
Sparse Core Ops, SparseCore 0:
  10.1 54.5 all-gather.8
  67.4 51.0 all-gather.6
  155.5 88.7 all-gather.10
where the time goes:
time: 263 us; the launch traced here: 262 us
  waiting for transfers between devices  107 us (41%)
  blocking collectives  57.9 us (22%)
  Pallas kernels  54.3 us (21%)
  between operations  14.5 us (6%)
  local copies, waits for them, and re-layouts  12.9 us (5%)
  starting transfers between devices  7.9 us (3%)
  other arithmetic  6.99 us (3%)
    all_gather x2, waiting for transfers between devices, body(): gathered.append(lax.all_gather(pair, CTX))  81.3 us
    all_to_all x1, blocking collectives, body(): maps = jnp.sum(lax.all_to_all(maps, DP_CTX, 0, 0, tiled=True), axis=0)  57.9 us
    pallas_call x1, Pallas kernels, body(): pl.pallas_call(student_kernel, grid_spec=pltpu.PrefetchScalarGridSpec(num...  24.1 us
    all_to_all x1, waiting for transfers between devices, body(): lax.all_to_all(jnp.broadcast_to(maps, (32, *maps.shape)), DP_CTX, 0, 0, t...  22.8 us
    pallas_call x1, Pallas kernels, body(): pl.pallas_call(local_kernel, grid=(HEADS // STEP,), in_specs=[by_head(TOK...  16.5 us
    pallas_call x2, Pallas kernels, body(): pl.pallas_call(teacher_kernel, grid_spec=pltpu.PrefetchScalarGridSpec(num...  9.33 us
    unnamed x24, local copies, waits for them, and re-layouts  8.83 us
  transfers between devices with their start and end apart: 7, of which 5 were waited for; matrix products, arithmetic and copies ran while one was open for 5% of the time, Pallas kernels for 8%

commit v1 on v0

v1 whole, which is shorter than its diff:
```python
import functools
import math

import jax
import jax.numpy as jnp
from jax import lax
from jax.experimental import pallas as pl
from jax.experimental.pallas import tpu as pltpu
from jax.sharding import Mesh
from jax.sharding import PartitionSpec as P


CTX = ("ctx_0", "ctx_1")
DP_CTX = ("dp", "ctx_0", "ctx_1")
F32 = jnp.float32
BF16 = jnp.bfloat16
LOG2E = 1.0 / math.log(2.0)
TOK = 256
WID = 128
GRP = 8
KVH = 2
HEADS = GRP * KVH
STEP = 2
WIDE = 8
TILE = 2
N_CTX = 16
SROWS = WID + 8


def split(x):
    hi = x.astype(BF16)
    return hi, (x - hi.astype(F32)).astype(BF16)


def dot(a, b, ca, cb):
    return lax.dot_general(a, b, (((ca,), (cb,)), ((), ())), preferred_element_type=F32)


def deep(a, b, ca, cb):
    ah, al = a
    bh, bl = b
    return dot(jnp.concatenate([ah, al], ca), jnp.concatenate([bh, bh], cb), ca, cb) + dot(ah, bl, ca, cb)


def wide(a, b, ca, cb):
    ah, al = a
    bh, bl = b
    n = bh.shape[1 - cb]
    both = dot(ah, jnp.concatenate([bh, bl], 1 - cb), ca, cb)
    return both[:, :n] + both[:, n:] + dot(al, bh, ca, cb)


def softmax(x):
    e = jnp.exp(x - jnp.max(x, axis=-1, keepdims=True))
    return e / jnp.sum(e, axis=-1, keepdims=True)


SOURCES = ((0, 3), (0, 1), (1, 0), (1, 3), (1, 1), (2, 0), (0, 2), (2, 3), (2, 1), (1, 2), (2, 2))


def bounds(docs):
    own = 4 * lax.axis_index("ctx_0") + lax.axis_index("ctx_1")
    first, last = 0, -1
    for j in range(N_CTX):
        first = first + (docs[j] < docs[own]).astype(jnp.int32)
        last = last + (docs[j] <= docs[own]).astype(jnp.int32)
    return first, own, last


def note_wanted(docs, flags, places):
    row, column = lax.axis_index("ctx_0"), lax.axis_index("ctx_1")
    own = 4 * row + column
    for k, place in enumerate(places):
        back, on = SOURCES[place]
        source = 4 * (row - back) + lax.rem(column + on, 4)
        seen = (source >= 0) & (source < own)
        flags[k] = (seen & (docs[jnp.maximum(source, 0)] == docs[own])).astype(jnp.int32)


def local_kernel(q_ref, k_ref, v_ref, w_ref, wk_ref, *refs):
    qf_ref, num_ref, acc_ref, stat_ref, a_ref, kf_ref, s_ref = refs[-7:]

    @pl.when(pl.program_id(0) == 0)
    def _():
        kf = softmax(deep(split(k_ref[0]), split(wk_ref[0]), 1, 0))
        kf_ref[0] = kf
        s_ref[0, :WID] = wide(split(kf), split(v_ref[0]), 0, 0)
        s_ref[0, WID:] = jnp.broadcast_to(jnp.sum(kf, axis=0, keepdims=True), (8, WID))

    k, v, kf = split(k_ref[0]), split(v_ref[0]), split(kf_ref[0])
    causal = lax.broadcasted_iota(jnp.int32, (TOK, TOK), 0) >= lax.broadcasted_iota(jnp.int32, (TOK, TOK), 1)
    lane = lax.broadcasted_iota(jnp.int32, (TOK, WID), 1)
    for i in range(STEP):
        q = q_ref[i]
        qf = softmax(deep(split(q), split(w_ref[i]), 1, 0))
        qf_ref[i] = qf
        a = jnp.where(causal, deep(split(qf), kf, 1, 1), 0.0)
        a_ref[i] = a
        num_ref[i] = wide(split(a), v, 1, 0)
        den = jnp.sum(a, axis=-1, keepdims=True)
        s = deep(split(q * (LOG2E / math.sqrt(WID))), k, 1, 1)
        s = jnp.where(causal, s, -1e30)
        m = jnp.max(s, axis=-1, keepdims=True)
        p = jnp.where(causal, jnp.exp2(s - m), 0.0)
        acc_ref[i] = wide(split(p), v, 1, 0)
        l = jnp.sum(p, axis=-1, keepdims=True)
        stat_ref[i] = jnp.where(lane == 0, m, jnp.where(lane == 1, l, den))


def attend_kernel(whole, halves, final, at, docs, q_ref, acc0_ref, stat_ref, *refs):
    count = whole + halves
    pieces, refs = refs[: whole + 2 * halves], refs[whole + 2 * halves :]
    if final:
        t_ref, sq_ref, flags, buf, sem, keys, values, qs, m_sc, l_sc, acc = refs
    else:
        acc_out, stat_out, flags, buf, sem, keys, values, qs, m_sc, l_sc, acc = refs
    g = pl.program_id(0)
    head = g // (GRP // WIDE)

    def copies(k):
        if k < whole:
            return [pltpu.make_async_copy(pieces[k], buf.at[k], sem.at[k, 0])]
        pair = pieces[whole + 2 * (k - whole) : whole + 2 * (k - whole) + 2]
        return [pltpu.make_async_copy(pair[h], buf.at[k, h], sem.at[k, h]) for h in range(KVH)]

    @pl.when(g == 0)
    def _():
        note_wanted(docs, flags, range(at, at + count))
        for k in range(count):

            @pl.when(flags[k] == 1)
            def _(k=k):
                for copy in copies(k):
                    copy.start()

    rows = TILE * TOK
    tiles = WIDE // TILE
    lane = lax.broadcasted_iota(jnp.int32, (rows, WID), 1)
    for i in range(tiles):
        here = pl.ds(i * rows, rows)
        q = q_ref[i * TILE : (i + 1) * TILE].reshape(rows, WID) * (LOG2E / math.sqrt(WID))
        hi, lo = split(q)
        qs[here, :WID] = hi
        qs[here, WID:] = lo
        stat = stat_ref[i * TILE : (i + 1) * TILE].reshape(rows, WID)
        m_sc[here, :] = jnp.broadcast_to(stat[:, 0:1], (rows, WID))
        l_sc[here, :] = jnp.where(lane == 1, stat, 0.0)
        acc[here, :] = acc0_ref[i * TILE : (i + 1) * TILE].reshape(rows, WID)

    @pl.when(g == 0)
    def _():
        for k in range(count):

            @pl.when(flags[k] == 1)
            def _(k=k):
                for copy in copies(k):
                    copy.wait()

        def divide(n, carry):
            k, h = n // KVH, n % KVH
            keys[k, h, :, :WID], keys[k, h, :, WID:] = split(buf[k, h, 0])
            values[k, h, :, :WID], values[k, h, :, WID:] = split(buf[k, h, 1])
            return carry

        lax.fori_loop(0, count * KVH, divide, 0)

    def visit(k, carry):
        @pl.when(flags[k] == 1)
        def _():
            kh, kl = keys[k, head, :, :WID], keys[k, head, :, WID:]
            v_both = values[k, head]
            k_twice = jnp.concatenate([kh, kh], 1)
            for i in range(tiles):
                here = pl.ds(i * rows, rows)
                q = qs[here, :]
                s = dot(q, k_twice, 1, 1) + dot(q[:, :WID], kl, 1, 1)
                m_old = m_sc[here, :]
                m_new = jnp.maximum(m_old, jnp.max(s, axis=-1, keepdims=True))
                p = jnp.exp2(s - jnp.concatenate([m_new, m_new], 1))
                fade = jnp.exp2(m_old - m_new)
                m_sc[here, :] = m_new
                l_sc[here, :] = fade * l_sc[here, :] + p[:, :WID] + p[:, WID:]
                ph, pl_ = split(p)
                both = dot(ph, v_both, 1, 0)
                acc[here, :] = (
                    fade * acc[here, :] + both[:, :WID] + both[:, WID:] + dot(pl_, v_both[:, :WID], 1, 0)
                )

        return carry

    lax.fori_loop(0, count, visit, 0)
    if not final:
        for i in range(tiles):
            here = pl.ds(i * rows, rows)
            acc_out[i * TILE : (i + 1) * TILE] = acc[here, :].reshape(TILE, TOK, WID)
            stat = stat_ref[i * TILE : (i + 1) * TILE].reshape(rows, WID)
            l = jnp.sum(l_sc[here, :], axis=-1, keepdims=True)
            stat = jnp.where(lane == 0, m_sc[here, :], jnp.where(lane == 1, l, stat))
            stat_out[i * TILE : (i + 1) * TILE] = stat.reshape(TILE, TOK, WID)
        return
    total = jnp.zeros((TOK, WID), F32)
    for i in range(tiles):
        here = pl.ds(i * rows, rows)
        t = acc[here, :] / jnp.sum(l_sc[here, :], axis=-1, keepdims=True)
        t_ref[i * TILE : (i + 1) * TILE] = t.reshape(TILE, TOK, WID)
        for k in range(TILE):
            part = t[k * TOK : (k + 1) * TOK]
            total = total + part * part
    line = jnp.sum(total, axis=-1, keepdims=True)
    line = jnp.transpose(jnp.broadcast_to(line, (TOK, WID)))[:8]

    @pl.when(g == 0)
    def _():
        sq_ref[...] = line

    @pl.when(g > 0)
    def _():
        sq_ref[...] += line


def student_kernel(
    docs, q_ref, qf_ref, num_ref, stat_ref, a_ref, t_ref, w_ref, v_ref, kf_ref, states_ref,
    sq0_ref, sq1_ref, sq2_ref, sq3_ref, gq_ref, mq_ref, gkf_ref, gv_ref, s_ref, prior_ref,
):
    step = pl.program_id(0)
    per = GRP // STEP

    @pl.when(step % per == 0)
    def _():
        gkf_ref[...] = jnp.zeros_like(gkf_ref)
        gv_ref[...] = jnp.zeros_like(gv_ref)
        s_ref[...] = jnp.zeros_like(s_ref)
        first, own, _ = bounds(docs)
        prior_ref[...] = lax.fori_loop(
            first, own, lambda j, held: held + states_ref[j, 0], jnp.zeros((SROWS, WID), F32)
        )

    prior = split(prior_ref[:WID])
    prior_n = prior_ref[WID : WID + 1]
    v, kf = split(v_ref[0]), split(kf_ref[0])
    squares = sq0_ref[...] + sq1_ref[...] + sq2_ref[...] + sq3_ref[...]
    mean = squares / (4 * HEADS * WID) + 1e-6
    scale = jnp.transpose(2.0 / mean)[:, 0:1]
    causal = lax.broadcasted_iota(jnp.int32, (TOK, TOK), 0) >= lax.broadcasted_iota(jnp.int32, (TOK, TOK), 1)
    for i in range(STEP):
        qf = qf_ref[i]
        qfs = split(qf)
        teacher = t_ref[i]
        num = num_ref[i] + deep(qfs, prior, 1, 0)
        den = stat_ref[i][:, 2:3] + jnp.sum(qf * prior_n, axis=-1, keepdims=True)
        inv = 1.0 / den
        student = num * inv
        gn = (student - teacher) * (scale * inv)
        gd = -jnp.sum(gn * student, axis=-1, keepdims=True)
        gns = split(gn)
        gs = jnp.where(causal, deep(gns, v, 1, 1) + gd, 0.0)
        gss = split(gs)
        gqf = deep(gns, prior, 1, 1) + gd * prior_n + wide(gss, kf, 1, 0)
        qlg = qf * (gqf - jnp.sum(qf * gqf, axis=-1, keepdims=True))
        qlgs = split(qlg)
        gq_ref[i] = deep(qlgs, split(w_ref[i]), 1, 1)
        mq_ref[i] = wide(split(q_ref[i]), qlgs, 0, 0)
        gkf_ref[0] += wide(gss, qfs, 0, 0)
        gv_ref[0] += wide(split(a_ref[i]), gns, 0, 0)
        s_ref[0, :WID] += wide(qfs, gns, 0, 0)
        s_ref[0, WID:] += jnp.broadcast_to(jnp.sum(qf * gd, axis=0, keepdims=True), (8, WID))


def key_map_kernel(docs, k_ref, kf_ref, gkf_ref, s_ref, wk_ref, *refs):
    pieces, (mk_ref, flags, buf, sem) = refs[:-4], refs[-4:]
    note_wanted(docs, flags, (0, 1, 2, 3, 4, 5, 7, 8, 6, 9, 10))
    state = [split(s_ref[h, :WID]) for h in range(KVH)]
    norm = [s_ref[h, WID : WID + 1] for h in range(KVH)]
    wk = [split(wk_ref[h]) for h in range(KVH)]

    def copies(k):
        if k < 8:
            return [pltpu.make_async_copy(pieces[k], buf.at[k], sem.at[k, 0])]
        return [pltpu.make_async_copy(pieces[2 * k - 8 + h], buf.at[k, h], sem.at[k, h]) for h in range(KVH)]

    for k in range(11):

        @pl.when(flags[k] == 1)
        def _(k=k):
            for copy in copies(k):
                copy.start()

    def logit_grad(feats, grad):
        return feats * (grad - jnp.sum(feats * grad, axis=-1, keepdims=True))

    for h in range(KVH):
        mk_ref[h] = wide(split(k_ref[h]), split(logit_grad(kf_ref[h], gkf_ref[h])), 0, 0)
    for k in range(11):

        @pl.when(flags[k] == 1)
        def _(k=k):
            for copy in copies(k):
                copy.wait()

    def visit(k, carry):
        @pl.when(flags[k] == 1)
        def _():
            for h in range(KVH):
                ks = split(buf[k, h, 0])
                feats = softmax(deep(ks, wk[h], 1, 0))
                grad = deep(split(buf[k, h, 1]), state[h], 1, 1) + norm[h]
                mk_ref[h] += wide(ks, split(logit_grad(feats, grad)), 0, 0)

        return carry

    lax.fori_loop(0, 11, visit, 0)


def later_kernel(docs, s_ref, gkf_ref, gv_ref, kf_ref, v_ref, wk_ref, gk_ref, out_ref):
    _, own, last = bounds(docs)
    for h in range(KVH):
        total = lax.fori_loop(
            own + 1, last + 1, lambda j, held: held + s_ref[j, h], jnp.zeros((SROWS, WID), F32)
        )
        state, norm = split(total[:WID]), total[WID : WID + 1]
        kf = kf_ref[h]
        gkf = gkf_ref[h] + deep(split(v_ref[h]), state, 1, 1) + norm
        out_ref[h] = gv_ref[h] + deep(split(kf), state, 1, 0)
        klg = kf * (gkf - jnp.sum(kf * gkf, axis=-1, keepdims=True))
        gk_ref[h] = deep(split(klg), split(wk_ref[h]), 1, 1)


def shape(*dims):
    return jax.ShapeDtypeStruct(dims, F32)


def full(*dims):
    return pl.BlockSpec(dims, lambda *_: (0,) * len(dims))


def params(limit=56):
    return pltpu.CompilerParams(vmem_limit_bytes=limit * 1024 * 1024)


def cost(us):
    return pl.CostEstimate(flops=int(us * 1e9), bytes_accessed=int(us * 3e5), transcendentals=0)


def body(queries, key_rows, value_rows, query_map, key_map, block_doc):
    keys = jnp.transpose(key_rows[0], (1, 0, 2))
    values = jnp.transpose(value_rows[0], (1, 0, 2))
    mine = jnp.stack([keys, values], 1)
    down = lambda x: lax.ppermute(x, "ctx_0", [(i, i + 1) for i in range(3)])
    right = lambda x: lax.ppermute(x, "ctx_1", [(i, (i + 1) % 4) for i in range(4)])
    left = lambda x: lax.ppermute(x, "ctx_1", [(i, (i - 1) % 4) for i in range(4)])
    docs = block_doc[0]
    q = jnp.transpose(queries[0], (1, 0, 2))
    per = GRP // STEP
    by_head = lambda *dims: pl.BlockSpec((STEP, *dims), lambda g, *_: (g, 0, 0))
    by_kv = lambda *dims: pl.BlockSpec((1, *dims), lambda g, *_: (g // per, 0, 0))

    any_spec = pl.BlockSpec(memory_space=pl.ANY)

    def local(h, held):
        part = lambda *dims: pl.BlockSpec((STEP, *dims), lambda g: (g + h * per, 0, 0))
        kv = lambda *dims: pl.BlockSpec((1, *dims), lambda g: (h, 0, 0))
        return pl.pallas_call(
            local_kernel,
            grid=(per,),
            in_specs=[part(TOK, WID), kv(TOK, WID), kv(TOK, WID), part(WID, WID), kv(WID, WID)]
            + [any_spec] * len(held),
            out_specs=[part(TOK, WID)] * 4 + [part(TOK, TOK), kv(TOK, WID), kv(SROWS, WID)],
            out_shape=[shape(HEADS, TOK, WID)] * 4
            + [shape(HEADS, TOK, TOK), shape(KVH, TOK, WID), shape(KVH, SROWS, WID)],
            input_output_aliases={5 + i: i for i in range(len(held))},
            compiler_params=params(),
            cost_estimate=cost(8),
            name="local",
        )(q, keys, values, query_map, key_map, *held)

    arrived = down(mine), right(mine), left(mine)
    held = local(0, ())
    (za, yp0, ym0), held = lax.optimization_barrier((arrived, held))
    zb, yp1, ym1 = down(za), right(za), left(za)
    yp2, ym2 = right(zb), left(zb)
    across = [(right(p[0]), left(m[1])) for p, m in ((yp0, ym0), (yp1, ym1), (yp2, ym2))]

    qf, num, acc, stat, a, kf, states = local(1, held)
    block_states = lax.all_gather(states, CTX)

    wide_head = lambda *dims: pl.BlockSpec((WIDE, *dims), lambda g, *_: (g, 0, 0))

    def attend(acc, stat, whole, halves, at, final, us):
        count = len(whole) + len(halves)
        return pl.pallas_call(
            functools.partial(attend_kernel, len(whole), len(halves), final, at),
            grid_spec=pltpu.PrefetchScalarGridSpec(
                num_scalar_prefetch=1,
                grid=(HEADS // WIDE,),
                in_specs=[wide_head(TOK, WID)] * 3 + [any_spec] * (len(whole) + 2 * len(halves)),
                out_specs=[wide_head(TOK, WID), full(8, TOK) if final else wide_head(TOK, WID)],
                scratch_shapes=[
                    pltpu.SMEM((count,), jnp.int32),
                    pltpu.VMEM((count, KVH, 2, TOK, WID), F32),
                    pltpu.SemaphoreType.DMA((count, KVH)),
                    pltpu.VMEM((count, KVH, TOK, 2 * WID), BF16),
                    pltpu.VMEM((count, KVH, TOK, 2 * WID), BF16),
                    pltpu.VMEM((WIDE * TOK, 2 * WID), BF16),
                ]
                + [pltpu.VMEM((WIDE * TOK, WID), F32)] * 3,
            ),
            out_shape=[shape(HEADS, TOK, WID), shape(8, TOK) if final else shape(HEADS, TOK, WID)],
            compiler_params=params(26),
            cost_estimate=cost(us),
            name="attend",
        )(docs, q, acc, stat, *whole, *[x for pair in halves for x in pair])

    acc, stat = attend(acc, stat, [yp0, ym0, za], [], 0, False, 14)
    acc, stat = attend(acc, stat, [yp1, ym1, zb], [across[0]], 3, False, 16)
    acc, stat = attend(acc, stat, [yp2, ym2], [across[1]], 7, False, 12)
    teacher, squares = attend(acc, stat, [], [across[2]], 10, True, 6)
    others = [lax.ppermute(squares, "head", [(i, (i + k) % 4) for i in range(4)]) for k in (1, 2, 3)]

    gq, mq, gkf, gv, states = pl.pallas_call(
        student_kernel,
        grid_spec=pltpu.PrefetchScalarGridSpec(
            num_scalar_prefetch=1,
            grid=(HEADS // STEP,),
            in_specs=[
                by_head(TOK, WID), by_head(TOK, WID), by_head(TOK, WID), by_head(TOK, WID), by_head(TOK, TOK),
                by_head(TOK, WID), by_head(WID, WID), by_kv(TOK, WID), by_kv(TOK, WID),
                pl.BlockSpec((N_CTX, 1, SROWS, WID), lambda g, *_: (0, g // per, 0, 0)),
                full(8, TOK), full(8, TOK), full(8, TOK), full(8, TOK),
            ],
            out_specs=[by_head(TOK, WID), by_head(WID, WID), by_kv(TOK, WID), by_kv(TOK, WID), by_kv(SROWS, WID)],
            scratch_shapes=[pltpu.VMEM((SROWS, WID), F32)],
        ),
        out_shape=[
            shape(HEADS, TOK, WID), shape(HEADS, WID, WID), shape(KVH, TOK, WID), shape(KVH, TOK, WID),
            shape(KVH, SROWS, WID),
        ],
        compiler_params=params(),
        cost_estimate=cost(25),
        name="student",
    )(docs, q, qf, num, stat, a, teacher, query_map, values, kf, block_states, squares, *others)

    all_states = lax.all_gather(states, CTX)
    share = lambda x: jnp.sum(lax.all_to_all(x.reshape(32, -1, WID), DP_CTX, 0, 0, tiled=True), axis=0)
    query_part = share(mq)
    mk = pl.pallas_call(
        key_map_kernel,
        grid_spec=pltpu.PrefetchScalarGridSpec(
            num_scalar_prefetch=1,
            grid=(1,),
            in_specs=[full(KVH, TOK, WID)] * 3 + [full(KVH, SROWS, WID), full(KVH, WID, WID)] + [any_spec] * 14,
            out_specs=full(KVH, WID, WID),
            scratch_shapes=[pltpu.SMEM((11,), jnp.int32), pltpu.VMEM((11, KVH, 2, TOK, WID), F32), pltpu.SemaphoreType.DMA((11, KVH))],
        ),
        out_shape=shape(KVH, WID, WID),
        compiler_params=params(),
        cost_estimate=cost(10),
        name="key_map",
    )(docs, keys, kf, gkf, states, key_map,
      yp0, ym0, za, yp1, ym1, zb, yp2, ym2, *[x for pair in across for x in pair])
    mk, query_part = lax.optimization_barrier((mk, query_part))
    parts = jnp.concatenate([query_part, share(mk)])
    maps = lax.all_to_all(jnp.broadcast_to(parts, (32, *parts.shape)), DP_CTX, 0, 0, tiled=True)
    rows = HEADS * WID // 32
    grad_keys, grad_values = pl.pallas_call(
        later_kernel,
        grid_spec=pltpu.PrefetchScalarGridSpec(
            num_scalar_prefetch=1,
            grid=(1,),
            in_specs=[full(N_CTX, KVH, SROWS, WID)] + [full(KVH, TOK, WID)] * 4 + [full(KVH, WID, WID)],
            out_specs=[full(KVH, TOK, WID)] * 2,
        ),
        out_shape=[shape(KVH, TOK, WID)] * 2,
        compiler_params=params(),
        name="later",
    )(docs, all_states, gkf, gv, kf, values, key_map)
    back = lambda x: jnp.transpose(x, (1, 0, 2))[None]
    return (back(gq), back(grad_keys), back(grad_values), maps[:, :rows].reshape(mq.shape), maps[:, rows:].reshape(mk.shape))


def solution(mesh):
    torus = Mesh(
        mesh.devices.reshape(mesh.shape["dp"], 4, 4, mesh.shape["head"]),
        ("dp", "ctx_0", "ctx_1", "head"),
    )
    rows = P("dp", CTX, "head", None)
    placed = (rows, rows, rows, P("head", None, None), P("head", None, None), P("dp", None))
    return jax.shard_map(
        body, mesh=torus, in_specs=placed, out_specs=(rows, rows, rows, placed[3], placed[4]), check_vma=False
    )
```

time: 263 us -> 221 us (0.84)
  waiting for transfers between devices: 107 us -> 53.3 us
  starting transfers between devices: 7.9 us -> 57.4 us
  blocking collectives: 57.9 us -> 12.9 us
  Pallas kernels: 54.3 us -> 62.1 us
  local copies, waits for them, and re-layouts: 12.9 us -> 20.2 us
  other arithmetic: 6.99 us -> 0.15 us
    all_gather x2 -> x1, waiting for transfers between devices: 81.3 us -> 0.01 us  [body(): block_states = lax.all_gather(states, CTX)]
    all_to_all x1, blocking collectives: 57.9 us -> 12.9 us  [body(): lax.all_to_all(x.reshape(32, -1, WID), DP_CTX, 0, 0, tiled=True)]
    ppermute x0 -> x14, starting transfers between devices: none -> 32.6 us  [the longest x6 24.3 us: body(): lax.ppermute(x, 'ctx_1', [(i, (i - 1) % 4) for i in range(4)])]
    ppermute x0 -> x14, waiting for transfers between devices: none -> 19.7 us  [the longest x6 15.9 us: body(): lax.ppermute(x, 'ctx_1', [(i, (i - 1) % 4) for i in range(4)])]
    all_to_all x1 -> x2, starting transfers between devices: 4.22 us -> 21 us  [the longest x1 16.5 us: body(): lax.all_to_all(x.reshape(32, -1, WID), DP_CTX, 0, 0, tiled=True)]
    pallas_call x3 -> x7, Pallas kernels: 25.9 us -> 34.8 us  [the longest x2 18.7 us: local(): pl.pallas_call(local_kernel, grid=(per,), in_specs=[part(TOK, WID), kv(TO...]
    all_to_all x1 -> x2, waiting for transfers between devices: 22.8 us -> 30.5 us  [the longest x1 15.4 us: body(): lax.all_to_all(jnp.broadcast_to(parts, (32, *parts.shape)), DP_CTX, 0, 0,...]
    unnamed x24 -> x48, local copies, waits for them, and re-layouts: 8.83 us -> 13.3 us
  transfers between devices with their start and end apart: 7 -> 21, of which waited for: 5 -> 7; matrix products, arithmetic and copies ran while one was open for 5% -> 4% of each run, Pallas kernels for 8% -> 16%
where the time goes in v1:
time: 221 us; the launch traced here: 220 us
  Pallas kernels  62.1 us (28%)
  starting transfers between devices  57.4 us (26%)
  waiting for transfers between devices  53.3 us (24%)
  local copies, waits for them, and re-layouts  20.2 us (9%)
  between operations  14.4 us (7%)
  blocking collectives  12.9 us (6%)
    ppermute x6, starting transfers between devices, body(): lax.ppermute(x, 'ctx_1', [(i, (i - 1) % 4) for i in range(4)])  24.3 us
    pallas_call x1, Pallas kernels, body(): pl.pallas_call(student_kernel, grid_spec=pltpu.PrefetchScalarGridSpec(num...  22.9 us
    pallas_call x2, Pallas kernels, local(): pl.pallas_call(local_kernel, grid=(per,), in_specs=[part(TOK, WID), kv(TO...  18.7 us
    all_to_all x1, starting transfers between devices, body(): lax.all_to_all(x.reshape(32, -1, WID), DP_CTX, 0, 0, tiled=True)  16.5 us
    ppermute x6, waiting for transfers between devices, body(): lax.ppermute(x, 'ctx_1', [(i, (i - 1) % 4) for i in range(4)])  15.9 us
    all_to_all x1, waiting for transfers between devices, body(): lax.all_to_all(jnp.broadcast_to(parts, (32, *parts.shape)), DP_CTX, 0, 0,...  15.4 us
    all_to_all x1, waiting for transfers between devices, body(): lax.all_to_all(x.reshape(32, -1, WID), DP_CTX, 0, 0, tiled=True)  15.1 us
    unnamed x48, local copies, waits for them, and re-layouts  13.3 us
  transfers between devices with their start and end apart: 21, of which 7 were waited for; matrix products, arithmetic and copies ran while one was open for 4% of the time, Pallas kernels for 16%

profile of v1, /device:TPU:1, one launch (start us, length us, event | category | flops | bytes accessed | tf_op | source)
XLA Modules:
  0.0 220.4 jit_solution(12017312498583678855)
XLA Ops:
  7.2 2.0 copy_bitcast_fusion.1
  9.3 3.6 %collective-permute-start.2 = (f32[2,2,256,128]{3,2,1,0:T(8,128)S(1)}, f32[2,2,256,128]{3,2,1,0:T(8,128)S(1)}, u32[]{:S(2)}, u32[]{:S(2)}) collective-permute-start(f32[2,2,256,128]{3,2,1,0:T(8,128)S(1)} %pad_maximum_fusion), channel_id=1, source_target_pairs={{0,12},{4,0},{8,4},{12,8},{1,13},{5,1},{9,5},{13,9},{2,14},{6,2},{... | collective-permute-start | bytes 1572872 | tf_op jit(solution)/shard_map/ppermute | solution.py:350
  12.9 4.4 %collective-permute-start = (f32[2,2,256,128]{3,2,1,0:T(8,128)S(1)}, f32[2,2,256,128]{3,2,1,0:T(8,128)}, u32[]{:S(2)}, u32[]{:S(2)}) collective-permute-start(f32[2,2,256,128]{3,2,1,0:T(8,128)S(1)} %pad_maximum_fusion), channel_id=1, source_target_pairs={{0,16},{16,32},{32,48},{1,17},{17,33},{33,49},{2,18},{18,34},{34,5... | collective-permute-start | bytes 1572872 | tf_op jit(solution)/shard_map/ppermute | solution.py:348
  17.3 2.0 copy.35
  19.2 9.4 %local.2 = (f32[16,256,128]{2,1,0:T(8,128)}, f32[16,256,128]{2,1,0:T(8,128)}, f32[16,256,128]{2,1,0:T(8,128)}, f32[16,256,128]{2,1,0:T(8,128)}, f32[16,256,256]{...) custom-call(f32[16,256,128]{2,1,0:T(8,128)} %bitcast.47, f32[2,256,128]{2,1,0:T(8,128)} %get-tuple-element.101.k_ref, ...), custom_call_target="tpu_custom_call" | custom-call | flops 8000000000 | bytes 2400000 | tf_op jit(solution)/shard_map/local/pallas_call | solution.py:362
  28.7 3.8 %collective-permute-start.5 = (f32[2,2,256,128]{3,2,1,0:T(8,128)}, f32[2,2,256,128]{3,2,1,0:T(8,128)}, u32[]{:S(2)}, u32[]{:S(2)}) collective-permute-start(f32[2,2,256,128]{3,2,1,0:T(8,128)} %collective-permute-done.refs_2_), channel_id=1, source_target_pairs={{0,16},{16,32},{32,48},{1,17},{17,33},{33,49},{2,18},{18,34},{34,5... | collective-permute-start | bytes 1572872 | tf_op jit(solution)/shard_map/ppermute | solution.py:348
  32.5 2.7 %collective-permute-start.4 = (f32[2,2,256,128]{3,2,1,0:T(8,128)}, f32[2,2,256,128]{3,2,1,0:T(8,128)}, u32[]{:S(2)}, u32[]{:S(2)}) collective-permute-start(f32[2,2,256,128]{3,2,1,0:T(8,128)} %collective-permute-done.refs_2_), channel_id=1, source_target_pairs={{0,12},{4,0},{8,4},{12,8},{1,13},{5,1},{9,5},{13,9},{2,14},{6,2},{... | collective-permute-start | bytes 1572872 | tf_op jit(solution)/shard_map/ppermute | solution.py:350
  35.2 9.4 %local.3 = (f32[16,256,128]{2,1,0:T(8,128)}, f32[16,256,128]{2,1,0:T(8,128)}, f32[16,256,128]{2,1,0:T(8,128)}, f32[16,256,128]{2,1,0:T(8,128)}, f32[16,256,256]{...) custom-call(f32[16,256,128]{2,1,0:T(8,128)} %bitcast.48, ...), custom_call_target="tpu_custom_call", output_to_operand_aliasing={{0}: (5, {}), {1}: (6, {}), {2}: (7, {}), {3}: (8, {}), {4}... | custom-call | flops 8000000000 | bytes 2400000 | tf_op jit(solution)/shard_map/local/pallas_call | solution.py:362
  44.7 2.7 %collective-permute-start.7 = (f32[2,256,128]{2,1,0:T(8,128)S(1)}, f32[2,256,128]{2,1,0:T(8,128)S(1)}, u32[]{:S(2)}, u32[]{:S(2)}) collective-permute-start(f32[2,256,128]{2,1,0:T(8,128)S(1)} %slice_bitcast_fusion.4), channel_id=1, source_target_pairs={{0,12},{4,0},{8,4},{12,8},{1,13},{5,1},{9,5},{13,9},{2,14},{6,2},{... | collective-permute-start | bytes 786440 | tf_op jit(solution)/shard_map/ppermute | solution.py:350
  47.5 1.6 copy-done.13
  49.0 1.6 copy-done.14
  50.6 3.2 %attend.4 = (f32[16,256,128]{2,1,0:T(8,128)S(1)}, f32[16,256,128]{2,1,0:T(8,128)S(1)}) custom-call(s32[16]{0:T(128)S(1)} %bitcast.57, f32[16,256,128]{2,1,0:T(8,128)S(1)} %bitcast.50, f32[16,256,128]{2,1,0:T(8,128)S(1)} %copy-done.13, f32[16,256,128]{2,1,0:T(8,128)S(1)} %copy-done.14, f32[2,2,256,128]{3,2,1,0:T(8,128)S(1)} %collective-permute-done.1.refs_0_, ...), custom_call_target="tpu_custom_call" | custom-call | flops 14000000000 | bytes 4200000 | tf_op jit(solution)/shard_map/attend/pallas_call | solution.py:390
  53.8 1.0 slice_bitcast_fusion.2
  54.8 9.1 %collective-permute-start.11 = (f32[2,256,128]{2,1,0:T(8,128)S(1)}, f32[2,256,128]{2,1,0:T(8,128)S(1)}, u32[]{:S(2)}, u32[]{:S(2)}) collective-permute-start(f32[2,256,128]{2,1,0:T(8,128)S(1)} %slice_bitcast_fusion.2), channel_id=1, source_target_pairs={{0,12},{4,0},{8,4},{12,8},{1,13},{5,1},{9,5},{13,9},{2,14},{6,2},{... | collective-permute-start | bytes 786440 | tf_op jit(solution)/shard_map/ppermute | solution.py:350
  63.9 1.0 slice_bitcast_fusion.3
  64.9 0.1 collective-permute-start.10
  65.0 2.7 %collective-permute-start.9 = (f32[2,2,256,128]{3,2,1,0:T(8,128)}, f32[2,2,256,128]{3,2,1,0:T(8,128)S(1)}, u32[]{:S(2)}, u32[]{:S(2)}) collective-permute-start(f32[2,2,256,128]{3,2,1,0:T(8,128)} %collective-permute-done.5.refs_2_.refs_5_), channel_id=1, source_target_pairs={{0,12},{4,0},{8,4},{12,8},{1,13},{5,1},{9,5},{13,9},{2,14},{6,2},{... | collective-permute-start | bytes 1572872 | tf_op jit(solution)/shard_map/ppermute | solution.py:350
  67.7 3.3 %attend.5 = (f32[16,256,128]{2,1,0:T(8,128)S(1)}, f32[16,256,128]{2,1,0:T(8,128)S(1)}) custom-call(s32[16]{0:T(128)S(1)} %bitcast.58, f32[16,256,128]{2,1,0:T(8,128)S(1)} %bitcast.51, f32[16,256,128]{2,1,0:T(8,128)S(1)} %get-tuple-element.67.acc0_ref, f32[16,256,128]{2,1,0:T(8,128)S(1)} %get-tuple-element.68.stat_ref, ...), custom_call_target="tpu_custom_call" | custom-call | flops 16000000000 | bytes 4800000 | tf_op jit(solution)/shard_map/attend/pallas_call | solution.py:390
  71.0 10.3 %collective-permute-done.9.refs_1_.refs_7_ = f32[2,2,256,128]{3,2,1,0:T(8,128)S(1)} collective-permute-done((f32[2,2,256,128]{3,2,1,0:T(8,128)}, f32[2,2,256,128]{3,2,1,0:T(8,128)S(1)}, u32[]{:S(2)}, u32[]{:S(2)}) %collective-permute-start.9) | collective-permute-done | bytes 524320 | tf_op jit(solution)/shard_map/ppermute | solution.py:350
  81.4 3.5 %collective-permute-start.13 = (f32[2,256,128]{2,1,0:T(8,128)S(1)}, f32[2,256,128]{2,1,0:T(8,128)S(1)}, u32[]{:S(2)}, u32[]{:S(2)}) collective-permute-start(f32[2,256,128]{2,1,0:T(8,128)S(1)} %slice_bitcast_fusion), channel_id=1, source_target_pairs={{0,12},{4,0},{8,4},{12,8},{1,13},{5,1},{9,5},{13,9},{2,14},{6,2},{... | collective-permute-start | bytes 786440 | tf_op jit(solution)/shard_map/ppermute | solution.py:350
  84.9 0.1 collective-permute-start.12
  85.0 3.2 %attend.6 = (f32[16,256,128]{2,1,0:T(8,128)S(1)}, f32[16,256,128]{2,1,0:T(8,128)S(1)}) custom-call(s32[16]{0:T(128)S(1)} %bitcast.59, f32[16,256,128]{2,1,0:T(8,128)S(1)} %bitcast.52, f32[16,256,128]{2,1,0:T(8,128)S(1)} %get-tuple-element.69.acc0_ref, f32[16,256,128]{2,1,0:T(8,128)S(1)} %get-tuple-element.70.stat_ref, ...), custom_call_target="tpu_custom_call" | custom-call | flops 12000000000 | bytes 3600000 | tf_op jit(solution)/shard_map/attend/pallas_call | solution.py:390
  88.2 5.5 %collective-permute-done.13.refs_1_.refs_13_ = f32[2,256,128]{2,1,0:T(8,128)S(1)} collective-permute-done((f32[2,256,128]{2,1,0:T(8,128)S(1)}, f32[2,256,128]{2,1,0:T(8,128)S(1)}, u32[]{:S(2)}, u32[]{:S(2)}) %collective-permute-start.13) | collective-permute-done | bytes 262176 | tf_op jit(solution)/shard_map/ppermute | solution.py:350
  93.8 3.8 %collective-permute-done.12.refs_0_.refs_12_ = f32[2,256,128]{2,1,0:T(8,128)S(1)} collective-permute-done((f32[2,256,128]{2,1,0:T(8,128)S(1)}, f32[2,256,128]{2,1,0:T(8,128)S(1)}, u32[]{:S(2)}, u32[]{:S(2)}) %collective-permute-start.12) | collective-permute-done | bytes 262176 | tf_op jit(solution)/shard_map/ppermute | solution.py:349
  97.6 3.0 %attend.7 = (f32[16,256,128]{2,1,0:T(8,128)S(1)}, f32[8,256]{1,0:T(8,128)S(1)}) custom-call(s32[16]{0:T(128)S(1)} %bitcast.60, f32[16,256,128]{2,1,0:T(8,128)S(1)} %bitcast.53, f32[16,256,128]{2,1,0:T(8,128)S(1)} %get-tuple-element.73.acc0_ref, f32[16,256,128]{2,1,0:T(8,128)S(1)} %get-tuple-element.71.stat_ref, ...), custom_call_target="tpu_custom_call" | custom-call | flops 6000000000 | bytes 1800000 | tf_op jit(solution)/shard_map/attend/pallas_call | solution.py:390
  100.6 1.3 copy-done.16
  101.9 2.5 %collective-permute-start.16 = (f32[8,256]{1,0:T(8,128)S(1)}, f32[8,256]{1,0:T(8,128)S(1)}, u32[]{:S(2)}, u32[]{:S(2)}) collective-permute-start(f32[8,256]{1,0:T(8,128)S(1)} %get-tuple-element.77.sq0_ref), channel_id=1, source_target_pairs={{0,3},{1,0},{2,1},{3,2},{4,7},{5,4},{6,5},{7,6},{8,11},{9,8},{10,9... | collective-permute-start | bytes 24584 | tf_op jit(solution)/shard_map/ppermute | solution.py:417
  104.4 0.5 collective-permute-start.15
  105.0 0.6 collective-permute-start.14
  105.6 2.9 %collective-permute-done.15.sq2_ref = f32[8,256]{1,0:T(8,128)S(1)} collective-permute-done((f32[8,256]{1,0:T(8,128)S(1)}, f32[8,256]{1,0:T(8,128)S(1)}, u32[]{:S(2)}, u32[]{:S(2)}) %collective-permute-start.15) | collective-permute-done | bytes 8224 | tf_op jit(solution)/shard_map/ppermute | solution.py:417
  108.4 0.2 collective-permute-done.14.sq1_ref
  108.7 0.3 copy-done.20
  109.0 0.2 copy-done.21
  109.3 22.9 %student.1 = (f32[16,256,128]{2,1,0:T(8,128)}, f32[16,128,128]{2,1,0:T(8,128)}, f32[2,256,128]{2,1,0:T(8,128)}, f32[2,256,128]{2,1,0:T(8,128)}, f32[2,136,128]{2,1,0:T(8,128)}) custom-call(s32[16]{0:T(128)} %bitcast.54, f32[16,256,128]{2,1,0:T(8,128)} %bitcast.49, f32[16,256,128]{2,1,0:T(8,128)} %get-tuple-element.60.qf_ref, ...), custom_call_target="tpu_custom_call" | custom-call | flops 24999999488 | bytes 7500000 | tf_op jit(solution)/shard_map/student/pallas_call | solution.py:419
  132.2 16.5 %all-to-all-start = ((f32[32,64,128]{2,1,0:T(8,128)}), f32[32,64,128]{2,1,0:T(8,128)S(1)}, u32[]{:S(2)}, u32[]{:S(2)}) async-start(f32[32,64,128]{2,1,0:T(8,128)} %bitcast.63), calls=%async_computation | async-start | bytes 2097152 | tf_op jit(solution)/shard_map/all_to_all | solution.py:443
  148.7 3.3 %key_map.1 = f32[2,128,128]{2,1,0:T(8,128)} custom-call(s32[16]{0:T(128)} %bitcast.55, f32[2,256,128]{2,1,0:T(8,128)} %get-tuple-element.101.k_ref, f32[2,256,128]{2,1,0:T(8,128)} %get-tuple-element.75.kf_ref, f32[2,256,128]{2,1,0:T(8,128)} %get-tuple-element.80.gkf_ref, f32[2,136,128]{2,1,0:T(8,128)} %get-tuple-element.79.s_ref, f32[2,128,128]{2,1,0:T(8,128)} %wk_ref.7, ...), custom_call_target="tpu_custom_call" | custom-call | flops 10000000000 | bytes 3000000 | tf_op jit(solution)/shard_map/key_map/pallas_call | solution.py:445
  152.1 15.1 %all-to-all-done = f32[32,64,128]{2,1,0:T(8,128)S(1)} async-done(((f32[32,64,128]{2,1,0:T(8,128)}), f32[32,64,128]{2,1,0:T(8,128)S(1)}, u32[]{:S(2)}, u32[]{:S(2)}) %all-to-all-start) | async-done | bytes 1048608 | tf_op jit(solution)/shard_map/all_to_all | solution.py:443
  167.1 0.1 reduce_sum.18
  167.2 12.9 %all_to_all.15 = f32[32,8,128]{2,1,0:T(8,128)S(1)} all-to-all(f32[32,8,128]{2,1,0:T(8,128)} %bitcast.68), channel_id=1, replica_groups=mesh['dp'=2,'ctx_0'=4,'ctx_1'=4,'head'=4] {'dp','ctx_0','ctx_1'}, dimensions={0} | all-to-all | bytes 262144 | tf_op jit(solution)/shard_map/all_to_all | solution.py:443
  180.2 1.1 broadcast_in_dim.15
  181.3 4.5 %all-to-all-start.2 = ((f32[32,72,128]{2,1,0:T(8,128)}), f32[32,72,128]{2,1,0:T(8,128)S(1)}, u32[]{:S(2)}, u32[]{:S(2)}) async-start(f32[32,72,128]{2,1,0:T(8,128)} %broadcast_in_dim.15), calls=%async_computation.2 | async-start | bytes 2359296 | tf_op jit(solution)/shard_map/all_to_all | solution.py:462
  185.8 2.5 %copy.27 = f32[1,256,16,128]{3,2,1,0:T(8,128)} copy(f32[1,256,16,128]{3,1,2,0:T(8,128)S(1)} %bitcast.62) | data formatting | bytes 4194304
  188.3 15.4 %all-to-all-done.2 = f32[32,72,128]{2,1,0:T(8,128)S(1)} async-done(((f32[32,72,128]{2,1,0:T(8,128)}), f32[32,72,128]{2,1,0:T(8,128)S(1)}, u32[]{:S(2)}, u32[]{:S(2)}) %all-to-all-start.2) | async-done | bytes 1179680 | tf_op jit(solution)/shard_map/all_to_all | solution.py:462
  203.7 0.7 slice.37
  204.4 1.1 slice.36
  205.5 4.4 %later.1 = (f32[2,256,128]{2,1,0:T(8,128)}, f32[2,256,128]{2,1,0:T(8,128)}) custom-call(s32[16]{0:T(128)} %bitcast.56, f32[16,2,136,128]{3,2,1,0:T(8,128)} %bitcast.61, f32[2,256,128]{2,1,0:T(8,128)} %get-tuple-element.80.gkf_ref, f32[2,256,128]{2,1,0:T(8,128)} %get-tuple-element.81.gv_ref, f32[2,256,128]{2,1,0:T(8,128)} %get-tuple-element.75.kf_ref, ...), custom_call_target="tpu_custom_call" | custom-call | tf_op jit(solution)/shard_map/later/pallas_call | solution.py:464
  209.9 1.9 copy.28
  211.7 1.9 copy.29
  (68 shorter events, 0.4 us)
Async XLA Ops:
  7.2 10.1 %copy-start.17 = (f32[1,256,16,128]{3,2,1,0:T(8,128)S(1)}, f32[1,256,16,128]{3,2,1,0:T(8,128)}, u32[]{:S(2)}) copy-start(f32[1,256,16,128]{3,2,1,0:T(8,128)} %param.6) | copy-start | bytes 6291460
  7.2 101.5 %all-gather.5.cloned.1.call-start = ((), (), s32[]{:S(2)}) async-start(), calls=%async_computation.3 | async-start | bytes 2367488 | tf_op jit(solution)/shard_map/all_gather | solution.py:384
  9.3 19.3 %collective-permute-start.2 = (f32[2,2,256,128]{3,2,1,0:T(8,128)S(1)}, f32[2,2,256,128]{3,2,1,0:T(8,128)S(1)}, u32[]{:S(2)}, u32[]{:S(2)}) collective-permute-start(f32[2,2,256,128]{3,2,1,0:T(8,128)S(1)} %pad_maximum_fusion), channel_id=1, source_target_pairs={{0,12},{4,0},{8,4},{12,8},{1,13},{5,1},{9,5},{13,9},{2,14},{6,2},{... | collective-permute-start | bytes 1572872 | tf_op jit(solution)/shard_map/ppermute | solution.py:350
  12.9 15.7 %collective-permute-start.1 = (f32[2,2,256,128]{3,2,1,0:T(8,128)S(1)}, f32[2,2,256,128]{3,2,1,0:T(8,128)S(1)}, u32[]{:S(2)}, u32[]{:S(2)}) collective-permute-start(f32[2,2,256,128]{3,2,1,0:T(8,128)S(1)} %pad_maximum_fusion), channel_id=1, source_target_pairs={{0,4},{4,8},{8,12},{12,0},{1,5},{5,9},{9,13},{13,1},{2,6},{6,10},{... | collective-permute-start | bytes 1572872 | tf_op jit(solution)/shard_map/ppermute | solution.py:349
  12.9 15.7 %collective-permute-start = (f32[2,2,256,128]{3,2,1,0:T(8,128)S(1)}, f32[2,2,256,128]{3,2,1,0:T(8,128)}, u32[]{:S(2)}, u32[]{:S(2)}) collective-permute-start(f32[2,2,256,128]{3,2,1,0:T(8,128)S(1)} %pad_maximum_fusion), channel_id=1, source_target_pairs={{0,16},{16,32},{32,48},{1,17},{17,33},{33,49},{2,18},{18,34},{34,5... | collective-permute-start | bytes 1572872 | tf_op jit(solution)/shard_map/ppermute | solution.py:348
  28.6 18.8 %copy-start.1 = (f32[2,2,256,128]{3,2,1,0:T(8,128)}, f32[2,2,256,128]{3,2,1,0:T(8,128)S(1)}, u32[]{:S(2)}) copy-start(f32[2,2,256,128]{3,2,1,0:T(8,128)S(1)} %collective-permute-done.2.refs_1_) | copy-start | bytes 1572868
  28.6 18.8 %copy-start.2 = (f32[2,2,256,128]{3,2,1,0:T(8,128)}, f32[2,2,256,128]{3,2,1,0:T(8,128)S(1)}, u32[]{:S(2)}) copy-start(f32[2,2,256,128]{3,2,1,0:T(8,128)S(1)} %collective-permute-done.1.refs_0_) | copy-start | bytes 1572868
  28.7 18.8 %copy-start = (f32[1,256,16,128]{3,1,2,0:T(8,128)S(1)}, f32[1,256,16,128]{3,1,2,0:T(8,128)}, u32[]{:S(2)}) copy-start(f32[1,256,16,128]{3,1,2,0:T(8,128)} %copy.35) | copy-start | bytes 6291460
  28.7 18.8 %copy-start.5 = (s32[1,16]{1,0:T(1,128)S(1)}, s32[1,16]{1,0:T(1,128)}, u32[]{:S(2)}) copy-start(s32[1,16]{1,0:T(1,128)} %param.11) | copy-start | bytes 196
  28.7 36.3 %collective-permute-start.5 = (f32[2,2,256,128]{3,2,1,0:T(8,128)}, f32[2,2,256,128]{3,2,1,0:T(8,128)}, u32[]{:S(2)}, u32[]{:S(2)}) collective-permute-start(f32[2,2,256,128]{3,2,1,0:T(8,128)} %collective-permute-done.refs_2_), channel_id=1, source_target_pairs={{0,16},{16,32},{32,48},{1,17},{17,33},{33,49},{2,18},{18,34},{34,5... | collective-permute-start | bytes 1572872 | tf_op jit(solution)/shard_map/ppermute | solution.py:348
  32.5 21.3 %collective-permute-start.4 = (f32[2,2,256,128]{3,2,1,0:T(8,128)}, f32[2,2,256,128]{3,2,1,0:T(8,128)}, u32[]{:S(2)}, u32[]{:S(2)}) collective-permute-start(f32[2,2,256,128]{3,2,1,0:T(8,128)} %collective-permute-done.refs_2_), channel_id=1, source_target_pairs={{0,12},{4,0},{8,4},{12,8},{1,13},{5,1},{9,5},{13,9},{2,14},{6,2},{... | collective-permute-start | bytes 1572872 | tf_op jit(solution)/shard_map/ppermute | solution.py:350
  35.2 28.7 %collective-permute-start.3 = (f32[2,2,256,128]{3,2,1,0:T(8,128)}, f32[2,2,256,128]{3,2,1,0:T(8,128)}, u32[]{:S(2)}, u32[]{:S(2)}) collective-permute-start(f32[2,2,256,128]{3,2,1,0:T(8,128)} %collective-permute-done.refs_2_), channel_id=1, source_target_pairs={{0,4},{4,8},{8,12},{12,0},{1,5},{5,9},{9,13},{13,1},{2,6},{6,10},{... | collective-permute-start | bytes 1572872 | tf_op jit(solution)/shard_map/ppermute | solution.py:349
  44.6 160.9 %all-gather.7.cloned.1.call-start = ((), (), s32[]{:S(2)}) async-start(), calls=%async_computation.4 | async-start | bytes 2367488 | tf_op jit(solution)/shard_map/all_gather | solution.py:442
  44.7 22.9 %collective-permute-start.7 = (f32[2,256,128]{2,1,0:T(8,128)S(1)}, f32[2,256,128]{2,1,0:T(8,128)S(1)}, u32[]{:S(2)}, u32[]{:S(2)}) collective-permute-start(f32[2,256,128]{2,1,0:T(8,128)S(1)} %slice_bitcast_fusion.4), channel_id=1, source_target_pairs={{0,12},{4,0},{8,4},{12,8},{1,13},{5,1},{9,5},{13,9},{2,14},{6,2},{... | collective-permute-start | bytes 786440 | tf_op jit(solution)/shard_map/ppermute | solution.py:350
  47.4 20.2 %collective-permute-start.6 = (f32[2,256,128]{2,1,0:T(8,128)S(1)}, f32[2,256,128]{2,1,0:T(8,128)S(1)}, u32[]{:S(2)}, u32[]{:S(2)}) collective-permute-start(f32[2,256,128]{2,1,0:T(8,128)S(1)} %slice_bitcast_fusion.5), channel_id=1, source_target_pairs={{0,4},{4,8},{8,12},{12,0},{1,5},{5,9},{9,13},{13,1},{2,6},{6,10},{... | collective-permute-start | bytes 786440 | tf_op jit(solution)/shard_map/ppermute | solution.py:349
  47.4 1.6 copy-start.13
  49.0 1.6 copy-start.14
  54.8 30.2 %collective-permute-start.11 = (f32[2,256,128]{2,1,0:T(8,128)S(1)}, f32[2,256,128]{2,1,0:T(8,128)S(1)}, u32[]{:S(2)}, u32[]{:S(2)}) collective-permute-start(f32[2,256,128]{2,1,0:T(8,128)S(1)} %slice_bitcast_fusion.2), channel_id=1, source_target_pairs={{0,12},{4,0},{8,4},{12,8},{1,13},{5,1},{9,5},{13,9},{2,14},{6,2},{... | collective-permute-start | bytes 786440 | tf_op jit(solution)/shard_map/ppermute | solution.py:350
  64.9 20.1 %collective-permute-start.10 = (f32[2,256,128]{2,1,0:T(8,128)S(1)}, f32[2,256,128]{2,1,0:T(8,128)S(1)}, u32[]{:S(2)}, u32[]{:S(2)}) collective-permute-start(f32[2,256,128]{2,1,0:T(8,128)S(1)} %slice_bitcast_fusion.3), channel_id=1, source_target_pairs={{0,4},{4,8},{8,12},{12,0},{1,5},{5,9},{9,13},{13,1},{2,6},{6,10},{... | collective-permute-start | bytes 786440 | tf_op jit(solution)/shard_map/ppermute | solution.py:349
  65.0 16.4 %collective-permute-start.9 = (f32[2,2,256,128]{3,2,1,0:T(8,128)}, f32[2,2,256,128]{3,2,1,0:T(8,128)S(1)}, u32[]{:S(2)}, u32[]{:S(2)}) collective-permute-start(f32[2,2,256,128]{3,2,1,0:T(8,128)} %collective-permute-done.5.refs_2_.refs_5_), channel_id=1, source_target_pairs={{0,12},{4,0},{8,4},{12,8},{1,13},{5,1},{9,5},{13,9},{2,14},{6,2},{... | collective-permute-start | bytes 1572872 | tf_op jit(solution)/shard_map/ppermute | solution.py:350
  67.6 3.4 %copy-start.6 = (f32[2,256,128]{2,1,0:T(8,128)}, f32[2,256,128]{2,1,0:T(8,128)S(1)}, u32[]{:S(2)}) copy-start(f32[2,256,128]{2,1,0:T(8,128)S(1)} %collective-permute-done.7.refs_4_.refs_9_) | copy-start | bytes 786436
  67.6 17.2 %collective-permute-start.8 = (f32[2,2,256,128]{3,2,1,0:T(8,128)}, f32[2,2,256,128]{3,2,1,0:T(8,128)S(1)}, u32[]{:S(2)}, u32[]{:S(2)}) collective-permute-start(f32[2,2,256,128]{3,2,1,0:T(8,128)} %collective-permute-done.5.refs_2_.refs_5_), channel_id=1, source_target_pairs={{0,4},{4,8},{8,12},{12,0},{1,5},{5,9},{9,13},{13,1},{2,6},{6,10},{... | collective-permute-start | bytes 1572872 | tf_op jit(solution)/shard_map/ppermute | solution.py:349
  67.7 3.4 %copy-start.7 = (f32[2,256,128]{2,1,0:T(8,128)}, f32[2,256,128]{2,1,0:T(8,128)S(1)}, u32[]{:S(2)}) copy-start(f32[2,256,128]{2,1,0:T(8,128)S(1)} %collective-permute-done.6.refs_3_.refs_8_) | copy-start | bytes 786436
  81.4 6.8 %copy-start.3 = (f32[2,2,256,128]{3,2,1,0:T(8,128)}, f32[2,2,256,128]{3,2,1,0:T(8,128)S(1)}, u32[]{:S(2)}) copy-start(f32[2,2,256,128]{3,2,1,0:T(8,128)S(1)} %collective-permute-done.9.refs_1_.refs_7_) | copy-start | bytes 1572868
  81.4 12.4 %collective-permute-start.13 = (f32[2,256,128]{2,1,0:T(8,128)S(1)}, f32[2,256,128]{2,1,0:T(8,128)S(1)}, u32[]{:S(2)}, u32[]{:S(2)}) collective-permute-start(f32[2,256,128]{2,1,0:T(8,128)S(1)} %slice_bitcast_fusion), channel_id=1, source_target_pairs={{0,12},{4,0},{8,4},{12,8},{1,13},{5,1},{9,5},{13,9},{2,14},{6,2},{... | collective-permute-start | bytes 786440 | tf_op jit(solution)/shard_map/ppermute | solution.py:350
  84.9 3.3 %copy-start.4 = (f32[2,2,256,128]{3,2,1,0:T(8,128)}, f32[2,2,256,128]{3,2,1,0:T(8,128)S(1)}, u32[]{:S(2)}) copy-start(f32[2,2,256,128]{3,2,1,0:T(8,128)S(1)} %collective-permute-done.8.refs_0_.refs_6_) | copy-start | bytes 1572868
  84.9 12.7 %collective-permute-start.12 = (f32[2,256,128]{2,1,0:T(8,128)S(1)}, f32[2,256,128]{2,1,0:T(8,128)S(1)}, u32[]{:S(2)}, u32[]{:S(2)}) collective-permute-start(f32[2,256,128]{2,1,0:T(8,128)S(1)} %slice_bitcast_fusion.1), channel_id=1, source_target_pairs={{0,4},{4,8},{8,12},{12,0},{1,5},{5,9},{9,13},{13,1},{2,6},{6,10},{... | collective-permute-start | bytes 786440 | tf_op jit(solution)/shard_map/ppermute | solution.py:349
  85.0 3.2 %copy-start.8 = (f32[2,256,128]{2,1,0:T(8,128)}, f32[2,256,128]{2,1,0:T(8,128)S(1)}, u32[]{:S(2)}) copy-start(f32[2,256,128]{2,1,0:T(8,128)S(1)} %collective-permute-done.11.refs_3_.refs_11_) | copy-start | bytes 786436
  85.0 3.2 %copy-start.9 = (f32[2,256,128]{2,1,0:T(8,128)}, f32[2,256,128]{2,1,0:T(8,128)S(1)}, u32[]{:S(2)}) copy-start(f32[2,256,128]{2,1,0:T(8,128)S(1)} %collective-permute-done.10.refs_2_.refs_10_) | copy-start | bytes 786436
  88.2 12.3 %copy-start.15 = (f32[16,256,128]{2,1,0:T(8,128)}, f32[16,256,128]{2,1,0:T(8,128)S(1)}, u32[]{:S(2)}) copy-start(f32[16,256,128]{2,1,0:T(8,128)S(1)} %get-tuple-element.71.stat_ref) | copy-start | bytes 6291460
  93.8 6.8 %copy-start.10 = (f32[2,256,128]{2,1,0:T(8,128)}, f32[2,256,128]{2,1,0:T(8,128)S(1)}, u32[]{:S(2)}) copy-start(f32[2,256,128]{2,1,0:T(8,128)S(1)} %collective-permute-done.13.refs_1_.refs_13_) | copy-start | bytes 786436
  97.6 3.1 %copy-start.11 = (f32[2,256,128]{2,1,0:T(8,128)}, f32[2,256,128]{2,1,0:T(8,128)S(1)}, u32[]{:S(2)}) copy-start(f32[2,256,128]{2,1,0:T(8,128)S(1)} %collective-permute-done.12.refs_0_.refs_12_) | copy-start | bytes 786436
  100.6 1.3 copy-start.16
  101.9 6.8 %copy-start.12 = (f32[8,256]{1,0:T(8,128)}, f32[8,256]{1,0:T(8,128)S(1)}, u32[]{:S(2)}) copy-start(f32[8,256]{1,0:T(8,128)S(1)} %get-tuple-element.77.sq0_ref) | copy-start | bytes 24580
  101.9 3.6 %collective-permute-start.16 = (f32[8,256]{1,0:T(8,128)S(1)}, f32[8,256]{1,0:T(8,128)S(1)}, u32[]{:S(2)}, u32[]{:S(2)}) collective-permute-start(f32[8,256]{1,0:T(8,128)S(1)} %get-tuple-element.77.sq0_ref), channel_id=1, source_target_pairs={{0,3},{1,0},{2,1},{3,2},{4,7},{5,4},{6,5},{7,6},{8,11},{9,8},{10,9... | collective-permute-start | bytes 24584 | tf_op jit(solution)/shard_map/ppermute | solution.py:417
  104.4 4.0 %collective-permute-start.15 = (f32[8,256]{1,0:T(8,128)S(1)}, f32[8,256]{1,0:T(8,128)S(1)}, u32[]{:S(2)}, u32[]{:S(2)}) collective-permute-start(f32[8,256]{1,0:T(8,128)S(1)} %get-tuple-element.77.sq0_ref), channel_id=1, source_target_pairs={{0,2},{1,3},{2,0},{3,1},{4,6},{5,7},{6,4},{7,5},{8,10},{9,11},{10,... | collective-permute-start | bytes 24584 | tf_op jit(solution)/shard_map/ppermute | solution.py:417
  105.0 3.7 %collective-permute-start.14 = (f32[8,256]{1,0:T(8,128)S(1)}, f32[8,256]{1,0:T(8,128)S(1)}, u32[]{:S(2)}, u32[]{:S(2)}) collective-permute-start(f32[8,256]{1,0:T(8,128)S(1)} %get-tuple-element.77.sq0_ref), channel_id=1, source_target_pairs={{0,1},{1,2},{2,3},{3,0},{4,5},{5,6},{6,7},{7,4},{8,9},{9,10},{10,1... | collective-permute-start | bytes 24584 | tf_op jit(solution)/shard_map/ppermute | solution.py:417
  105.6 3.1 %copy-start.19 = (f32[8,256]{1,0:T(8,128)}, f32[8,256]{1,0:T(8,128)S(1)}, u32[]{:S(2)}) copy-start(f32[8,256]{1,0:T(8,128)S(1)} %collective-permute-done.16.sq3_ref) | copy-start | bytes 24580
  108.4 0.6 copy-start.20
  108.7 0.6 copy-start.21
  132.2 35.0 %all-to-all-start = ((f32[32,64,128]{2,1,0:T(8,128)}), f32[32,64,128]{2,1,0:T(8,128)S(1)}, u32[]{:S(2)}, u32[]{:S(2)}) async-start(f32[32,64,128]{2,1,0:T(8,128)} %bitcast.63), calls=%async_computation | async-start | bytes 2097152 | tf_op jit(solution)/shard_map/all_to_all | solution.py:443
  167.2 18.6 %copy-start.18 = (f32[16,256,128]{2,1,0:T(8,128)S(1)}, f32[16,256,128]{2,1,0:T(8,128)}, u32[]{:S(2)}) copy-start(f32[16,256,128]{2,1,0:T(8,128)} %get-tuple-element.78) | copy-start | bytes 6291460
  181.3 22.4 %all-to-all-start.2 = ((f32[32,72,128]{2,1,0:T(8,128)}), f32[32,72,128]{2,1,0:T(8,128)S(1)}, u32[]{:S(2)}, u32[]{:S(2)}) async-start(f32[32,72,128]{2,1,0:T(8,128)} %broadcast_in_dim.15), calls=%async_computation.2 | async-start | bytes 2359296 | tf_op jit(solution)/shard_map/all_to_all | solution.py:462
Sparse Core Ops, SparseCore 0:
  44.7 52.2 all-gather.4
  132.3 56.3 all-gather.6

commit v2 on v1

--- a/solution.py
+++ b/solution.py
@@ -20,7 +20,8 @@
 GRP = 8
 KVH = 2
 HEADS = GRP * KVH
-STEP = 2
+STEP = 4
+EARLY = 4
 WIDE = 8
 TILE = 2
 N_CTX = 16
@@ -52,7 +53,7 @@
 
 def softmax(x):
     e = jnp.exp(x - jnp.max(x, axis=-1, keepdims=True))
-    return e / jnp.sum(e, axis=-1, keepdims=True)
+    return e / row_sum(e)
 
 
 SOURCES = ((0, 3), (0, 1), (1, 0), (1, 3), (1, 1), (2, 0), (0, 2), (2, 3), (2, 1), (1, 2), (2, 2))
@@ -77,6 +78,18 @@
         flags[k] = (seen & (docs[jnp.maximum(source, 0)] == docs[own])).astype(jnp.int32)
 
 
+HEAD_ROWS = [slice(i * TOK, (i + 1) * TOK) for i in range(GRP)]
+
+
+def stacked_mask(heads):
+    row = lax.broadcasted_iota(jnp.int32, (heads * TOK, TOK), 0)
+    return lax.rem(row, TOK) >= lax.broadcasted_iota(jnp.int32, (heads * TOK, TOK), 1)
+
+
+def row_sum(x):
+    return dot(jnp.concatenate(split(x), 1), jnp.ones((2 * WID, WID), BF16), 1, 0)
+
+
 def local_kernel(q_ref, k_ref, v_ref, w_ref, wk_ref, *refs):
     qf_ref, num_ref, acc_ref, stat_ref, a_ref, kf_ref, s_ref = refs[-7:]
 
@@ -88,23 +101,26 @@
         s_ref[0, WID:] = jnp.broadcast_to(jnp.sum(kf, axis=0, keepdims=True), (8, WID))
 
     k, v, kf = split(k_ref[0]), split(v_ref[0]), split(kf_ref[0])
-    causal = lax.broadcasted_iota(jnp.int32, (TOK, TOK), 0) >= lax.broadcasted_iota(jnp.int32, (TOK, TOK), 1)
-    lane = lax.broadcasted_iota(jnp.int32, (TOK, WID), 1)
-    for i in range(STEP):
-        q = q_ref[i]
-        qf = softmax(deep(split(q), split(w_ref[i]), 1, 0))
-        qf_ref[i] = qf
-        a = jnp.where(causal, deep(split(qf), kf, 1, 1), 0.0)
-        a_ref[i] = a
-        num_ref[i] = wide(split(a), v, 1, 0)
-        den = jnp.sum(a, axis=-1, keepdims=True)
-        s = deep(split(q * (LOG2E / math.sqrt(WID))), k, 1, 1)
-        s = jnp.where(causal, s, -1e30)
-        m = jnp.max(s, axis=-1, keepdims=True)
-        p = jnp.where(causal, jnp.exp2(s - m), 0.0)
-        acc_ref[i] = wide(split(p), v, 1, 0)
-        l = jnp.sum(p, axis=-1, keepdims=True)
-        stat_ref[i] = jnp.where(lane == 0, m, jnp.where(lane == 1, l, den))
+    rows = EARLY * TOK
+    causal = stacked_mask(EARLY)
+    lane = lax.broadcasted_iota(jnp.int32, (rows, WID), 1)
+    whole = lambda x: x.reshape(EARLY, TOK, x.shape[-1])
+    q = q_ref[...].reshape(rows, WID)
+    qh, ql = split(q)
+    logits = [deep((qh[at], ql[at]), split(w_ref[i]), 1, 0) for i, at in enumerate(HEAD_ROWS[:EARLY])]
+    qf = softmax(jnp.concatenate(logits, 0))
+    qf_ref[...] = whole(qf)
+    a = jnp.where(causal, deep(split(qf), kf, 1, 1), 0.0)
+    a_ref[...] = whole(a)
+    num_ref[...] = whole(wide(split(a), v, 1, 0))
+    den = jnp.sum(a, axis=-1, keepdims=True)
+    s = deep(split(q * (LOG2E / math.sqrt(WID))), k, 1, 1)
+    s = jnp.where(causal, s, -1e30)
+    m = jnp.max(s, axis=-1, keepdims=True)
+    p = jnp.where(causal, jnp.exp2(s - m), 0.0)
+    acc_ref[...] = whole(wide(split(p), v, 1, 0))
+    l = jnp.sum(p, axis=-1, keepdims=True)
+    stat_ref[...] = whole(jnp.where(lane == 0, m, jnp.where(lane == 1, l, den)))
 
 
 def attend_kernel(whole, halves, final, at, docs, q_ref, acc0_ref, stat_ref, *refs):
@@ -136,16 +152,20 @@
     rows = TILE * TOK
     tiles = WIDE // TILE
     lane = lax.broadcasted_iota(jnp.int32, (rows, WID), 1)
-    for i in range(tiles):
-        here = pl.ds(i * rows, rows)
-        q = q_ref[i * TILE : (i + 1) * TILE].reshape(rows, WID) * (LOG2E / math.sqrt(WID))
-        hi, lo = split(q)
+
+    def take_up(i, carry):
+        here = pl.ds(pl.multiple_of(i * rows, rows), rows)
+        some = pl.ds(i * TILE, TILE)
+        hi, lo = split(q_ref[some].reshape(rows, WID) * (LOG2E / math.sqrt(WID)))
         qs[here, :WID] = hi
         qs[here, WID:] = lo
-        stat = stat_ref[i * TILE : (i + 1) * TILE].reshape(rows, WID)
+        stat = stat_ref[some].reshape(rows, WID)
         m_sc[here, :] = jnp.broadcast_to(stat[:, 0:1], (rows, WID))
         l_sc[here, :] = jnp.where(lane == 1, stat, 0.0)
-        acc[here, :] = acc0_ref[i * TILE : (i + 1) * TILE].reshape(rows, WID)
+        acc[here, :] = acc0_ref[some].reshape(rows, WID)
+        return carry
+
+    lax.fori_loop(0, tiles, take_up, 0)
 
     @pl.when(g == 0)
     def _():
@@ -190,13 +210,17 @@
 
     lax.fori_loop(0, count, visit, 0)
     if not final:
-        for i in range(tiles):
-            here = pl.ds(i * rows, rows)
-            acc_out[i * TILE : (i + 1) * TILE] = acc[here, :].reshape(TILE, TOK, WID)
-            stat = stat_ref[i * TILE : (i + 1) * TILE].reshape(rows, WID)
+
+        def put_down(i, carry):
+            here = pl.ds(pl.multiple_of(i * rows, rows), rows)
+            some = pl.ds(i * TILE, TILE)
+            acc_out[some] = acc[here, :].reshape(TILE, TOK, WID)
             l = jnp.sum(l_sc[here, :], axis=-1, keepdims=True)
-            stat = jnp.where(lane == 0, m_sc[here, :], jnp.where(lane == 1, l, stat))
-            stat_out[i * TILE : (i + 1) * TILE] = stat.reshape(TILE, TOK, WID)
+            stat = jnp.where(lane == 1, l, stat_ref[some].reshape(rows, WID))
+            stat_out[some] = jnp.where(lane == 0, m_sc[here, :], stat).reshape(TILE, TOK, WID)
+            return carry
+
+        lax.fori_loop(0, tiles, put_down, 0)
         return
     total = jnp.zeros((TOK, WID), F32)
     for i in range(tiles):
@@ -220,7 +244,7 @@
 
 def student_kernel(
     docs, q_ref, qf_ref, num_ref, stat_ref, a_ref, t_ref, w_ref, v_ref, kf_ref, states_ref,
-    sq0_ref, sq1_ref, sq2_ref, sq3_ref, gq_ref, mq_ref, gkf_ref, gv_ref, s_ref, prior_ref,
+    sq0_ref, sq1_ref, sq2_ref, sq3_ref, gq_ref, mq_ref, gkf_ref, gv_ref, s_ref, prior_ref, scale_ref, both_ref,
 ):
     step = pl.program_id(0)
     per = GRP // STEP
@@ -235,39 +259,50 @@
             first, own, lambda j, held: held + states_ref[j, 0], jnp.zeros((SROWS, WID), F32)
         )
 
-    prior = split(prior_ref[:WID])
+        both_ref[:, :WID] = prior_ref[:WID]
+        both_ref[:, WID:] = jnp.transpose(jnp.broadcast_to(prior_ref[WID : WID + 1], (WID, WID)))
+
+    @pl.when(step == 0)
+    def _():
+        squares = sq0_ref[...] + sq1_ref[...] + sq2_ref[...] + sq3_ref[...]
+        mean = squares / (4 * HEADS * WID) + 1e-6
+        scale_ref[...] = jnp.broadcast_to(jnp.transpose(2.0 / mean)[:, 0:1], (TOK, WID))
+
+    both = split(both_ref[...])
+    prior = both[0][:, :WID], both[1][:, :WID]
     prior_n = prior_ref[WID : WID + 1]
     v, kf = split(v_ref[0]), split(kf_ref[0])
-    squares = sq0_ref[...] + sq1_ref[...] + sq2_ref[...] + sq3_ref[...]
-    mean = squares / (4 * HEADS * WID) + 1e-6
-    scale = jnp.transpose(2.0 / mean)[:, 0:1]
-    causal = lax.broadcasted_iota(jnp.int32, (TOK, TOK), 0) >= lax.broadcasted_iota(jnp.int32, (TOK, TOK), 1)
-    for i in range(STEP):
-        qf = qf_ref[i]
-        qfs = split(qf)
-        teacher = t_ref[i]
-        num = num_ref[i] + deep(qfs, prior, 1, 0)
-        den = stat_ref[i][:, 2:3] + jnp.sum(qf * prior_n, axis=-1, keepdims=True)
-        inv = 1.0 / den
-        student = num * inv
-        gn = (student - teacher) * (scale * inv)
-        gd = -jnp.sum(gn * student, axis=-1, keepdims=True)
-        gns = split(gn)
-        gs = jnp.where(causal, deep(gns, v, 1, 1) + gd, 0.0)
-        gss = split(gs)
-        gqf = deep(gns, prior, 1, 1) + gd * prior_n + wide(gss, kf, 1, 0)
-        qlg = qf * (gqf - jnp.sum(qf * gqf, axis=-1, keepdims=True))
-        qlgs = split(qlg)
-        gq_ref[i] = deep(qlgs, split(w_ref[i]), 1, 1)
-        mq_ref[i] = wide(split(q_ref[i]), qlgs, 0, 0)
-        gkf_ref[0] += wide(gss, qfs, 0, 0)
-        gv_ref[0] += wide(split(a_ref[i]), gns, 0, 0)
-        s_ref[0, :WID] += wide(qfs, gns, 0, 0)
-        s_ref[0, WID:] += jnp.broadcast_to(jnp.sum(qf * gd, axis=0, keepdims=True), (8, WID))
+    scale = jnp.concatenate([scale_ref[...]] * STEP, 0)
+    rows = STEP * TOK
+    causal = stacked_mask(STEP)
+    flat = lambda ref: ref[...].reshape(rows, ref.shape[-1])
+    qf = flat(qf_ref)
+    qfs = split(qf)
+    carried = deep(qfs, both, 1, 0)
+    num = flat(num_ref) + carried[:, :WID]
+    den = flat(stat_ref)[:, 2:3] + carried[:, WID:]
+    inv = 1.0 / den
+    student = num * inv
+    gn = (student - flat(t_ref)) * (scale * inv)
+    gd = -row_sum(gn * student)
+    gns = split(gn)
+    gs = jnp.where(causal, deep(gns, v, 1, 1) + jnp.concatenate([gd, gd], 1), 0.0)
+    gss = split(gs)
+    gqf = deep(gns, prior, 1, 1) + gd * prior_n + wide(gss, kf, 1, 0)
+    qlg = qf * (gqf - row_sum(qf * gqf))
+    qlh, qll = split(qlg)
+    for i, at in enumerate(HEAD_ROWS[:STEP]):
+        part = (qlh[at], qll[at])
+        gq_ref[i] = deep(part, split(w_ref[i]), 1, 1)
+        mq_ref[i] = wide(split(q_ref[i]), part, 0, 0)
+    gkf_ref[0] += wide(gss, qfs, 0, 0)
+    gv_ref[0] += wide(split(flat(a_ref)), gns, 0, 0)
+    s_ref[0, :WID] += wide(qfs, gns, 0, 0)
+    s_ref[0, WID:] += jnp.broadcast_to(jnp.sum(qf * gd, axis=0, keepdims=True), (8, WID))
 
 
 def key_map_kernel(docs, k_ref, kf_ref, gkf_ref, s_ref, wk_ref, *refs):
-    pieces, (mk_ref, flags, buf, sem) = refs[:-4], refs[-4:]
+    pieces, (mk_ref, flags, order, buf, sem) = refs[:-5], refs[-5:]
     note_wanted(docs, flags, (0, 1, 2, 3, 4, 5, 7, 8, 6, 9, 10))
     state = [split(s_ref[h, :WID]) for h in range(KVH)]
     norm = [s_ref[h, WID : WID + 1] for h in range(KVH)]
@@ -286,7 +321,7 @@
                 copy.start()
 
     def logit_grad(feats, grad):
-        return feats * (grad - jnp.sum(feats * grad, axis=-1, keepdims=True))
+        return feats * (grad - row_sum(feats * grad))
 
     for h in range(KVH):
         mk_ref[h] = wide(split(k_ref[h]), split(logit_grad(kf_ref[h], gkf_ref[h])), 0, 0)
@@ -297,18 +332,26 @@
             for copy in copies(k):
                 copy.wait()
 
-    def visit(k, carry):
-        @pl.when(flags[k] == 1)
-        def _():
-            for h in range(KVH):
-                ks = split(buf[k, h, 0])
-                feats = softmax(deep(ks, wk[h], 1, 0))
-                grad = deep(split(buf[k, h, 1]), state[h], 1, 1) + norm[h]
-                mk_ref[h] += wide(ks, split(logit_grad(feats, grad)), 0, 0)
-
+    count = jnp.int32(0)
+    for k in range(11):
+        order[count] = k
+        count = count + flags[k]
+
+    def visit(n, carry):
+        one = order[2 * n]
+        full_pair = 2 * n + 1 < count
+        two = jnp.where(full_pair, order[jnp.minimum(2 * n + 1, 11)], one)
+        row = lax.broadcasted_iota(jnp.int32, (2 * TOK, WID), 0)
+        kept = (row < TOK) | full_pair
+        for h in range(KVH):
+            ks = split(jnp.concatenate([buf[one, h, 0], buf[two, h, 0]], 0))
+            vs = split(jnp.concatenate([buf[one, h, 1], buf[two, h, 1]], 0))
+            feats = softmax(deep(ks, wk[h], 1, 0))
+            grad = deep(vs, state[h], 1, 1) + norm[h]
+            mk_ref[h] += wide(ks, split(jnp.where(kept, logit_grad(feats, grad), 0.0)), 0, 0)
         return carry
 
-    lax.fori_loop(0, 11, visit, 0)
+    lax.fori_loop(0, (count + 1) // 2, visit, 0)
 
 
 def later_kernel(docs, s_ref, gkf_ref, gv_ref, kf_ref, v_ref, wk_ref, gk_ref, out_ref):
@@ -321,7 +364,7 @@
         kf = kf_ref[h]
         gkf = gkf_ref[h] + deep(split(v_ref[h]), state, 1, 1) + norm
         out_ref[h] = gv_ref[h] + deep(split(kf), state, 1, 0)
-        klg = kf * (gkf - jnp.sum(kf * gkf, axis=-1, keepdims=True))
+        klg = kf * (gkf - row_sum(kf * gkf))
         gk_ref[h] = deep(split(klg), split(wk_ref[h]), 1, 1)
 
 
@@ -357,11 +400,11 @@
     any_spec = pl.BlockSpec(memory_space=pl.ANY)
 
     def local(h, held):
-        part = lambda *dims: pl.BlockSpec((STEP, *dims), lambda g: (g + h * per, 0, 0))
+        part = lambda *dims: pl.BlockSpec((EARLY, *dims), lambda g: (g + h * (GRP // EARLY), 0, 0))
         kv = lambda *dims: pl.BlockSpec((1, *dims), lambda g: (h, 0, 0))
         return pl.pallas_call(
             local_kernel,
-            grid=(per,),
+            grid=(GRP // EARLY,),
             in_specs=[part(TOK, WID), kv(TOK, WID), kv(TOK, WID), part(WID, WID), kv(WID, WID)]
             + [any_spec] * len(held),
             out_specs=[part(TOK, WID)] * 4 + [part(TOK, TOK), kv(TOK, WID), kv(SROWS, WID)],
@@ -428,7 +471,9 @@
                 full(8, TOK), full(8, TOK), full(8, TOK), full(8, TOK),
             ],
             out_specs=[by_head(TOK, WID), by_head(WID, WID), by_kv(TOK, WID), by_kv(TOK, WID), by_kv(SROWS, WID)],
-            scratch_shapes=[pltpu.VMEM((SROWS, WID), F32)],
+            scratch_shapes=[
+                pltpu.VMEM((SROWS, WID), F32), pltpu.VMEM((TOK, WID), F32), pltpu.VMEM((WID, 2 * WID), F32),
+            ],
         ),
         out_shape=[
             shape(HEADS, TOK, WID), shape(HEADS, WID, WID), shape(KVH, TOK, WID), shape(KVH, TOK, WID),
@@ -449,7 +494,7 @@
             grid=(1,),
             in_specs=[full(KVH, TOK, WID)] * 3 + [full(KVH, SROWS, WID), full(KVH, WID, WID)] + [any_spec] * 14,
             out_specs=full(KVH, WID, WID),
-            scratch_shapes=[pltpu.SMEM((11,), jnp.int32), pltpu.VMEM((11, KVH, 2, TOK, WID), F32), pltpu.SemaphoreType.DMA((11, KVH))],
+            scratch_shapes=[pltpu.SMEM((11,), jnp.int32), pltpu.SMEM((12,), jnp.int32), pltpu.VMEM((11, KVH, 2, TOK, WID), F32), pltpu.SemaphoreType.DMA((11, KVH))],
         ),
         out_shape=shape(KVH, WID, WID),
         compiler_params=params(),

time: 221 us -> 215 us (0.973)
  Pallas kernels: 62.1 us -> 54.8 us
    pallas_call x1, Pallas kernels: 22.9 us -> 16.4 us  [body(): pl.pallas_call(student_kernel, grid_spec=pltpu.PrefetchScalarGridSpec(num...]
    pallas_call x2, Pallas kernels: 18.7 us -> 15.2 us  [local(): pl.pallas_call(local_kernel, grid=(GRP // EARLY,), in_specs=[part(TOK, WI...]
    pallas_call x4, Pallas kernels: 12.7 us -> 15.2 us  [attend(): pl.pallas_call(functools.partial(attend_kernel, len(whole), len(halves),...]
where the time goes in v2:
time: 215 us; the launch traced here: 214 us
  starting transfers between devices  59 us (27%)
  Pallas kernels  54.8 us (25%)
  waiting for transfers between devices  51.7 us (24%)
  local copies, waits for them, and re-layouts  20.2 us (9%)
  between operations  14.4 us (7%)
  blocking collectives  13.4 us (6%)
    ppermute x6, starting transfers between devices, body(): lax.ppermute(x, 'ctx_1', [(i, (i - 1) % 4) for i in range(4)])  24 us
    all_to_all x1, starting transfers between devices, body(): lax.all_to_all(x.reshape(32, -1, WID), DP_CTX, 0, 0, tiled=True)  17.2 us
    pallas_call x1, Pallas kernels, body(): pl.pallas_call(student_kernel, grid_spec=pltpu.PrefetchScalarGridSpec(num...  16.4 us
    all_to_all x1, waiting for transfers between devices, body(): lax.all_to_all(jnp.broadcast_to(parts, (32, *parts.shape)), DP_CTX, 0, 0,...  15.4 us
    pallas_call x2, Pallas kernels, local(): pl.pallas_call(local_kernel, grid=(GRP // EARLY,), in_specs=[part(TOK, WI...  15.2 us
    pallas_call x4, Pallas kernels, attend(): pl.pallas_call(functools.partial(attend_kernel, len(whole), len(halves),...  15.2 us
    all_to_all x1, waiting for transfers between devices, body(): lax.all_to_all(x.reshape(32, -1, WID), DP_CTX, 0, 0, tiled=True)  14.9 us
    ppermute x6, waiting for transfers between devices, body(): lax.ppermute(x, 'ctx_1', [(i, (i - 1) % 4) for i in range(4)])  14.5 us
  transfers between devices with their start and end apart: 21, of which 7 were waited for; matrix products, arithmetic and copies ran while one was open for 4% of the time, Pallas kernels for 16%

profile of v2, /device:TPU:1, one launch (start us, length us, event | category | flops | bytes accessed | tf_op | source)
XLA Modules:
  0.0 213.7 jit_solution(6561311459736068787)
XLA Ops:
  7.2 2.0 copy_bitcast_fusion.1
  9.3 3.6 %collective-permute-start.2 = (f32[2,2,256,128]{3,2,1,0:T(8,128)S(1)}, f32[2,2,256,128]{3,2,1,0:T(8,128)S(1)}, u32[]{:S(2)}, u32[]{:S(2)}) collective-permute-start(f32[2,2,256,128]{3,2,1,0:T(8,128)S(1)} %pad_maximum_fusion), channel_id=1, source_target_pairs={{0,12},{4,0},{8,4},{12,8},{1,13},{5,1},{9,5},{13,9},{2,14},{6,2},{... | collective-permute-start | bytes 1572872 | tf_op jit(solution)/shard_map/ppermute | solution.py:393
  12.9 4.4 %collective-permute-start = (f32[2,2,256,128]{3,2,1,0:T(8,128)S(1)}, f32[2,2,256,128]{3,2,1,0:T(8,128)}, u32[]{:S(2)}, u32[]{:S(2)}) collective-permute-start(f32[2,2,256,128]{3,2,1,0:T(8,128)S(1)} %pad_maximum_fusion), channel_id=1, source_target_pairs={{0,16},{16,32},{32,48},{1,17},{17,33},{33,49},{2,18},{18,34},{34,5... | collective-permute-start | bytes 1572872 | tf_op jit(solution)/shard_map/ppermute | solution.py:391
  17.3 2.0 copy.35
  19.2 7.6 %local.2 = (f32[16,256,128]{2,1,0:T(8,128)}, f32[16,256,128]{2,1,0:T(8,128)}, f32[16,256,128]{2,1,0:T(8,128)}, f32[16,256,128]{2,1,0:T(8,128)}, f32[16,256,256]{...) custom-call(f32[16,256,128]{2,1,0:T(8,128)} %bitcast.47, f32[2,256,128]{2,1,0:T(8,128)} %get-tuple-element.101.k_ref, ...), custom_call_target="tpu_custom_call" | custom-call | flops 8000000000 | bytes 2400000 | tf_op jit(solution)/shard_map/local/pallas_call | solution.py:405
  26.9 5.0 %collective-permute-start.5 = (f32[2,2,256,128]{3,2,1,0:T(8,128)}, f32[2,2,256,128]{3,2,1,0:T(8,128)}, u32[]{:S(2)}, u32[]{:S(2)}) collective-permute-start(f32[2,2,256,128]{3,2,1,0:T(8,128)} %collective-permute-done.refs_2_), channel_id=1, source_target_pairs={{0,16},{16,32},{32,48},{1,17},{17,33},{33,49},{2,18},{18,34},{34,5... | collective-permute-start | bytes 1572872 | tf_op jit(solution)/shard_map/ppermute | solution.py:391
  31.9 2.4 %collective-permute-start.4 = (f32[2,2,256,128]{3,2,1,0:T(8,128)}, f32[2,2,256,128]{3,2,1,0:T(8,128)}, u32[]{:S(2)}, u32[]{:S(2)}) collective-permute-start(f32[2,2,256,128]{3,2,1,0:T(8,128)} %collective-permute-done.refs_2_), channel_id=1, source_target_pairs={{0,12},{4,0},{8,4},{12,8},{1,13},{5,1},{9,5},{13,9},{2,14},{6,2},{... | collective-permute-start | bytes 1572872 | tf_op jit(solution)/shard_map/ppermute | solution.py:393
  34.3 7.6 %local.3 = (f32[16,256,128]{2,1,0:T(8,128)}, f32[16,256,128]{2,1,0:T(8,128)}, f32[16,256,128]{2,1,0:T(8,128)}, f32[16,256,128]{2,1,0:T(8,128)}, f32[16,256,256]{...) custom-call(f32[16,256,128]{2,1,0:T(8,128)} %bitcast.48, ...), custom_call_target="tpu_custom_call", output_to_operand_aliasing={{0}: (5, {}), {1}: (6, {}), {2}: (7, {}), {3}: (8, {}), {4}... | custom-call | flops 8000000000 | bytes 2400000 | tf_op jit(solution)/shard_map/local/pallas_call | solution.py:405
  42.1 2.7 %collective-permute-start.7 = (f32[2,256,128]{2,1,0:T(8,128)S(1)}, f32[2,256,128]{2,1,0:T(8,128)S(1)}, u32[]{:S(2)}, u32[]{:S(2)}) collective-permute-start(f32[2,256,128]{2,1,0:T(8,128)S(1)} %slice_bitcast_fusion.4), channel_id=1, source_target_pairs={{0,12},{4,0},{8,4},{12,8},{1,13},{5,1},{9,5},{13,9},{2,14},{6,2},{... | collective-permute-start | bytes 786440 | tf_op jit(solution)/shard_map/ppermute | solution.py:393
  44.9 1.6 copy-done.13
  46.4 1.6 copy-done.14
  48.0 3.9 %attend.4 = (f32[16,256,128]{2,1,0:T(8,128)S(1)}, f32[16,256,128]{2,1,0:T(8,128)S(1)}) custom-call(s32[16]{0:T(128)S(1)} %bitcast.57, f32[16,256,128]{2,1,0:T(8,128)S(1)} %bitcast.50, f32[16,256,128]{2,1,0:T(8,128)S(1)} %copy-done.13, f32[16,256,128]{2,1,0:T(8,128)S(1)} %copy-done.14, f32[2,2,256,128]{3,2,1,0:T(8,128)S(1)} %collective-permute-done.1.refs_0_, ...), custom_call_target="tpu_custom_call" | custom-call | flops 14000000000 | bytes 4200000 | tf_op jit(solution)/shard_map/attend/pallas_call | solution.py:433
  51.9 1.0 slice_bitcast_fusion.2
  52.9 9.1 %collective-permute-start.11 = (f32[2,256,128]{2,1,0:T(8,128)S(1)}, f32[2,256,128]{2,1,0:T(8,128)S(1)}, u32[]{:S(2)}, u32[]{:S(2)}) collective-permute-start(f32[2,256,128]{2,1,0:T(8,128)S(1)} %slice_bitcast_fusion.2), channel_id=1, source_target_pairs={{0,12},{4,0},{8,4},{12,8},{1,13},{5,1},{9,5},{13,9},{2,14},{6,2},{... | collective-permute-start | bytes 786440 | tf_op jit(solution)/shard_map/ppermute | solution.py:393
  62.0 1.0 slice_bitcast_fusion.3
  63.0 0.1 collective-permute-start.10
  63.1 2.7 %collective-permute-start.9 = (f32[2,2,256,128]{3,2,1,0:T(8,128)}, f32[2,2,256,128]{3,2,1,0:T(8,128)S(1)}, u32[]{:S(2)}, u32[]{:S(2)}) collective-permute-start(f32[2,2,256,128]{3,2,1,0:T(8,128)} %collective-permute-done.5.refs_2_.refs_5_), channel_id=1, source_target_pairs={{0,12},{4,0},{8,4},{12,8},{1,13},{5,1},{9,5},{13,9},{2,14},{6,2},{... | collective-permute-start | bytes 1572872 | tf_op jit(solution)/shard_map/ppermute | solution.py:393
  65.8 4.1 %attend.5 = (f32[16,256,128]{2,1,0:T(8,128)S(1)}, f32[16,256,128]{2,1,0:T(8,128)S(1)}) custom-call(s32[16]{0:T(128)S(1)} %bitcast.58, f32[16,256,128]{2,1,0:T(8,128)S(1)} %bitcast.51, f32[16,256,128]{2,1,0:T(8,128)S(1)} %get-tuple-element.67.acc0_ref, f32[16,256,128]{2,1,0:T(8,128)S(1)} %get-tuple-element.68.stat_ref, ...), custom_call_target="tpu_custom_call" | custom-call | flops 16000000000 | bytes 4800000 | tf_op jit(solution)/shard_map/attend/pallas_call | solution.py:433
  69.9 9.6 %collective-permute-done.9.refs_1_.refs_7_ = f32[2,2,256,128]{3,2,1,0:T(8,128)S(1)} collective-permute-done((f32[2,2,256,128]{3,2,1,0:T(8,128)}, f32[2,2,256,128]{3,2,1,0:T(8,128)S(1)}, u32[]{:S(2)}, u32[]{:S(2)}) %collective-permute-start.9) | collective-permute-done | bytes 524320 | tf_op jit(solution)/shard_map/ppermute | solution.py:393
  79.5 3.5 %collective-permute-start.13 = (f32[2,256,128]{2,1,0:T(8,128)S(1)}, f32[2,256,128]{2,1,0:T(8,128)S(1)}, u32[]{:S(2)}, u32[]{:S(2)}) collective-permute-start(f32[2,256,128]{2,1,0:T(8,128)S(1)} %slice_bitcast_fusion), channel_id=1, source_target_pairs={{0,12},{4,0},{8,4},{12,8},{1,13},{5,1},{9,5},{13,9},{2,14},{6,2},{... | collective-permute-start | bytes 786440 | tf_op jit(solution)/shard_map/ppermute | solution.py:393
  83.0 0.1 collective-permute-start.12
  83.1 3.9 %attend.6 = (f32[16,256,128]{2,1,0:T(8,128)S(1)}, f32[16,256,128]{2,1,0:T(8,128)S(1)}) custom-call(s32[16]{0:T(128)S(1)} %bitcast.59, f32[16,256,128]{2,1,0:T(8,128)S(1)} %bitcast.52, f32[16,256,128]{2,1,0:T(8,128)S(1)} %get-tuple-element.69.acc0_ref, f32[16,256,128]{2,1,0:T(8,128)S(1)} %get-tuple-element.70.stat_ref, ...), custom_call_target="tpu_custom_call" | custom-call | flops 12000000000 | bytes 3600000 | tf_op jit(solution)/shard_map/attend/pallas_call | solution.py:433
  87.1 4.9 %collective-permute-done.13.refs_1_.refs_13_ = f32[2,256,128]{2,1,0:T(8,128)S(1)} collective-permute-done((f32[2,256,128]{2,1,0:T(8,128)S(1)}, f32[2,256,128]{2,1,0:T(8,128)S(1)}, u32[]{:S(2)}, u32[]{:S(2)}) %collective-permute-start.13) | collective-permute-done | bytes 262176 | tf_op jit(solution)/shard_map/ppermute | solution.py:393
  92.0 3.8 %collective-permute-done.12.refs_0_.refs_12_ = f32[2,256,128]{2,1,0:T(8,128)S(1)} collective-permute-done((f32[2,256,128]{2,1,0:T(8,128)S(1)}, f32[2,256,128]{2,1,0:T(8,128)S(1)}, u32[]{:S(2)}, u32[]{:S(2)}) %collective-permute-start.12) | collective-permute-done | bytes 262176 | tf_op jit(solution)/shard_map/ppermute | solution.py:392
  95.7 3.3 %attend.7 = (f32[16,256,128]{2,1,0:T(8,128)S(1)}, f32[8,256]{1,0:T(8,128)S(1)}) custom-call(s32[16]{0:T(128)S(1)} %bitcast.60, f32[16,256,128]{2,1,0:T(8,128)S(1)} %bitcast.53, f32[16,256,128]{2,1,0:T(8,128)S(1)} %get-tuple-element.73.acc0_ref, f32[16,256,128]{2,1,0:T(8,128)S(1)} %get-tuple-element.71.stat_ref, ...), custom_call_target="tpu_custom_call" | custom-call | flops 6000000000 | bytes 1800000 | tf_op jit(solution)/shard_map/attend/pallas_call | solution.py:433
  99.1 1.3 copy-done.16
  100.4 2.5 %collective-permute-start.16 = (f32[8,256]{1,0:T(8,128)S(1)}, f32[8,256]{1,0:T(8,128)S(1)}, u32[]{:S(2)}, u32[]{:S(2)}) collective-permute-start(f32[8,256]{1,0:T(8,128)S(1)} %get-tuple-element.77.sq0_ref), channel_id=1, source_target_pairs={{0,3},{1,0},{2,1},{3,2},{4,7},{5,4},{6,5},{7,6},{8,11},{9,8},{10,9... | collective-permute-start | bytes 24584 | tf_op jit(solution)/shard_map/ppermute | solution.py:460
  102.9 0.5 collective-permute-start.15
  103.5 0.6 collective-permute-start.14
  104.1 2.9 %collective-permute-done.15.sq2_ref = f32[8,256]{1,0:T(8,128)S(1)} collective-permute-done((f32[8,256]{1,0:T(8,128)S(1)}, f32[8,256]{1,0:T(8,128)S(1)}, u32[]{:S(2)}, u32[]{:S(2)}) %collective-permute-start.15) | collective-permute-done | bytes 8224 | tf_op jit(solution)/shard_map/ppermute | solution.py:460
  107.0 0.2 collective-permute-done.14.sq1_ref
  107.2 0.4 copy-done.20
  107.5 0.2 copy-done.21
  107.8 16.4 %student.1 = (f32[16,256,128]{2,1,0:T(8,128)}, f32[16,128,128]{2,1,0:T(8,128)}, f32[2,256,128]{2,1,0:T(8,128)}, f32[2,256,128]{2,1,0:T(8,128)}, f32[2,136,128]{2,1,0:T(8,128)}) custom-call(s32[16]{0:T(128)} %bitcast.54, f32[16,256,128]{2,1,0:T(8,128)} %bitcast.49, f32[16,256,128]{2,1,0:T(8,128)} %get-tuple-element.60.qf_ref, ...), custom_call_target="tpu_custom_call" | custom-call | flops 24999999488 | bytes 7500000 | tf_op jit(solution)/shard_map/student/pallas_call | solution.py:462
  124.2 17.2 %all-to-all-start = ((f32[32,64,128]{2,1,0:T(8,128)}), f32[32,64,128]{2,1,0:T(8,128)S(1)}, u32[]{:S(2)}, u32[]{:S(2)}) async-start(f32[32,64,128]{2,1,0:T(8,128)} %bitcast.63), calls=%async_computation | async-start | bytes 2097152 | tf_op jit(solution)/shard_map/all_to_all | solution.py:488
  141.5 3.5 %key_map.1 = f32[2,128,128]{2,1,0:T(8,128)} custom-call(s32[16]{0:T(128)} %bitcast.55, f32[2,256,128]{2,1,0:T(8,128)} %get-tuple-element.101.k_ref, f32[2,256,128]{2,1,0:T(8,128)} %get-tuple-element.75.kf_ref, f32[2,256,128]{2,1,0:T(8,128)} %get-tuple-element.80.gkf_ref, f32[2,136,128]{2,1,0:T(8,128)} %get-tuple-element.79.s_ref, f32[2,128,128]{2,1,0:T(8,128)} %wk_ref.7, ...), custom_call_target="tpu_custom_call" | custom-call | flops 10000000000 | bytes 3000000 | tf_op jit(solution)/shard_map/key_map/pallas_call | solution.py:490
  145.0 14.9 %all-to-all-done = f32[32,64,128]{2,1,0:T(8,128)S(1)} async-done(((f32[32,64,128]{2,1,0:T(8,128)}), f32[32,64,128]{2,1,0:T(8,128)S(1)}, u32[]{:S(2)}, u32[]{:S(2)}) %all-to-all-start) | async-done | bytes 1048608 | tf_op jit(solution)/shard_map/all_to_all | solution.py:488
  159.9 0.1 reduce_sum.18
  160.0 13.4 %all_to_all.15 = f32[32,8,128]{2,1,0:T(8,128)S(1)} all-to-all(f32[32,8,128]{2,1,0:T(8,128)} %bitcast.68), channel_id=1, replica_groups=mesh['dp'=2,'ctx_0'=4,'ctx_1'=4,'head'=4] {'dp','ctx_0','ctx_1'}, dimensions={0} | all-to-all | bytes 262144 | tf_op jit(solution)/shard_map/all_to_all | solution.py:488
  173.4 1.1 broadcast_in_dim.15
  174.5 4.5 %all-to-all-start.2 = ((f32[32,72,128]{2,1,0:T(8,128)}), f32[32,72,128]{2,1,0:T(8,128)S(1)}, u32[]{:S(2)}, u32[]{:S(2)}) async-start(f32[32,72,128]{2,1,0:T(8,128)} %broadcast_in_dim.15), calls=%async_computation.2 | async-start | bytes 2359296 | tf_op jit(solution)/shard_map/all_to_all | solution.py:507
  179.0 2.5 %copy.27 = f32[1,256,16,128]{3,2,1,0:T(8,128)} copy(f32[1,256,16,128]{3,1,2,0:T(8,128)S(1)} %bitcast.62) | data formatting | bytes 4194304
  181.6 15.4 %all-to-all-done.2 = f32[32,72,128]{2,1,0:T(8,128)S(1)} async-done(((f32[32,72,128]{2,1,0:T(8,128)}), f32[32,72,128]{2,1,0:T(8,128)S(1)}, u32[]{:S(2)}, u32[]{:S(2)}) %all-to-all-start.2) | async-done | bytes 1179680 | tf_op jit(solution)/shard_map/all_to_all | solution.py:507
  196.9 0.7 slice.37
  197.6 1.1 slice.36
  198.7 4.4 %later.1 = (f32[2,256,128]{2,1,0:T(8,128)}, f32[2,256,128]{2,1,0:T(8,128)}) custom-call(s32[16]{0:T(128)} %bitcast.56, f32[16,2,136,128]{3,2,1,0:T(8,128)} %bitcast.61, f32[2,256,128]{2,1,0:T(8,128)} %get-tuple-element.80.gkf_ref, f32[2,256,128]{2,1,0:T(8,128)} %get-tuple-element.81.gv_ref, f32[2,256,128]{2,1,0:T(8,128)} %get-tuple-element.75.kf_ref, ...), custom_call_target="tpu_custom_call" | custom-call | tf_op jit(solution)/shard_map/later/pallas_call | solution.py:509
  203.1 1.9 copy.28
  205.0 1.9 copy.29
  (68 shorter events, 0.4 us)
Async XLA Ops:
  7.2 10.1 %copy-start.17 = (f32[1,256,16,128]{3,2,1,0:T(8,128)S(1)}, f32[1,256,16,128]{3,2,1,0:T(8,128)}, u32[]{:S(2)}) copy-start(f32[1,256,16,128]{3,2,1,0:T(8,128)} %param.6) | copy-start | bytes 6291460
  7.2 100.0 %all-gather.5.cloned.1.call-start = ((), (), s32[]{:S(2)}) async-start(), calls=%async_computation.3 | async-start | bytes 2367488 | tf_op jit(solution)/shard_map/all_gather | solution.py:427
  9.3 17.5 %collective-permute-start.2 = (f32[2,2,256,128]{3,2,1,0:T(8,128)S(1)}, f32[2,2,256,128]{3,2,1,0:T(8,128)S(1)}, u32[]{:S(2)}, u32[]{:S(2)}) collective-permute-start(f32[2,2,256,128]{3,2,1,0:T(8,128)S(1)} %pad_maximum_fusion), channel_id=1, source_target_pairs={{0,12},{4,0},{8,4},{12,8},{1,13},{5,1},{9,5},{13,9},{2,14},{6,2},{... | collective-permute-start | bytes 1572872 | tf_op jit(solution)/shard_map/ppermute | solution.py:393
  12.9 13.9 %collective-permute-start.1 = (f32[2,2,256,128]{3,2,1,0:T(8,128)S(1)}, f32[2,2,256,128]{3,2,1,0:T(8,128)S(1)}, u32[]{:S(2)}, u32[]{:S(2)}) collective-permute-start(f32[2,2,256,128]{3,2,1,0:T(8,128)S(1)} %pad_maximum_fusion), channel_id=1, source_target_pairs={{0,4},{4,8},{8,12},{12,0},{1,5},{5,9},{9,13},{13,1},{2,6},{6,10},{... | collective-permute-start | bytes 1572872 | tf_op jit(solution)/shard_map/ppermute | solution.py:392
  12.9 13.9 %collective-permute-start = (f32[2,2,256,128]{3,2,1,0:T(8,128)S(1)}, f32[2,2,256,128]{3,2,1,0:T(8,128)}, u32[]{:S(2)}, u32[]{:S(2)}) collective-permute-start(f32[2,2,256,128]{3,2,1,0:T(8,128)S(1)} %pad_maximum_fusion), channel_id=1, source_target_pairs={{0,16},{16,32},{32,48},{1,17},{17,33},{33,49},{2,18},{18,34},{34,5... | collective-permute-start | bytes 1572872 | tf_op jit(solution)/shard_map/ppermute | solution.py:391
  26.8 18.0 %copy-start.1 = (f32[2,2,256,128]{3,2,1,0:T(8,128)}, f32[2,2,256,128]{3,2,1,0:T(8,128)S(1)}, u32[]{:S(2)}) copy-start(f32[2,2,256,128]{3,2,1,0:T(8,128)S(1)} %collective-permute-done.2.refs_1_) | copy-start | bytes 1572868
  26.8 18.0 %copy-start.2 = (f32[2,2,256,128]{3,2,1,0:T(8,128)}, f32[2,2,256,128]{3,2,1,0:T(8,128)S(1)}, u32[]{:S(2)}) copy-start(f32[2,2,256,128]{3,2,1,0:T(8,128)S(1)} %collective-permute-done.1.refs_0_) | copy-start | bytes 1572868
  26.9 18.0 %copy-start = (f32[1,256,16,128]{3,1,2,0:T(8,128)S(1)}, f32[1,256,16,128]{3,1,2,0:T(8,128)}, u32[]{:S(2)}) copy-start(f32[1,256,16,128]{3,1,2,0:T(8,128)} %copy.35) | copy-start | bytes 6291460
  26.9 18.0 %copy-start.5 = (s32[1,16]{1,0:T(1,128)S(1)}, s32[1,16]{1,0:T(1,128)}, u32[]{:S(2)}) copy-start(s32[1,16]{1,0:T(1,128)} %param.11) | copy-start | bytes 196
  26.9 36.2 %collective-permute-start.5 = (f32[2,2,256,128]{3,2,1,0:T(8,128)}, f32[2,2,256,128]{3,2,1,0:T(8,128)}, u32[]{:S(2)}, u32[]{:S(2)}) collective-permute-start(f32[2,2,256,128]{3,2,1,0:T(8,128)} %collective-permute-done.refs_2_), channel_id=1, source_target_pairs={{0,16},{16,32},{32,48},{1,17},{17,33},{33,49},{2,18},{18,34},{34,5... | collective-permute-start | bytes 1572872 | tf_op jit(solution)/shard_map/ppermute | solution.py:391
  31.9 20.0 %collective-permute-start.4 = (f32[2,2,256,128]{3,2,1,0:T(8,128)}, f32[2,2,256,128]{3,2,1,0:T(8,128)}, u32[]{:S(2)}, u32[]{:S(2)}) collective-permute-start(f32[2,2,256,128]{3,2,1,0:T(8,128)} %collective-permute-done.refs_2_), channel_id=1, source_target_pairs={{0,12},{4,0},{8,4},{12,8},{1,13},{5,1},{9,5},{13,9},{2,14},{6,2},{... | collective-permute-start | bytes 1572872 | tf_op jit(solution)/shard_map/ppermute | solution.py:393
  34.3 27.7 %collective-permute-start.3 = (f32[2,2,256,128]{3,2,1,0:T(8,128)}, f32[2,2,256,128]{3,2,1,0:T(8,128)}, u32[]{:S(2)}, u32[]{:S(2)}) collective-permute-start(f32[2,2,256,128]{3,2,1,0:T(8,128)} %collective-permute-done.refs_2_), channel_id=1, source_target_pairs={{0,4},{4,8},{8,12},{12,0},{1,5},{5,9},{9,13},{13,1},{2,6},{6,10},{... | collective-permute-start | bytes 1572872 | tf_op jit(solution)/shard_map/ppermute | solution.py:392
  42.0 156.7 %all-gather.7.cloned.1.call-start = ((), (), s32[]{:S(2)}) async-start(), calls=%async_computation.4 | async-start | bytes 2367488 | tf_op jit(solution)/shard_map/all_gather | solution.py:487
  42.1 23.7 %collective-permute-start.7 = (f32[2,256,128]{2,1,0:T(8,128)S(1)}, f32[2,256,128]{2,1,0:T(8,128)S(1)}, u32[]{:S(2)}, u32[]{:S(2)}) collective-permute-start(f32[2,256,128]{2,1,0:T(8,128)S(1)} %slice_bitcast_fusion.4), channel_id=1, source_target_pairs={{0,12},{4,0},{8,4},{12,8},{1,13},{5,1},{9,5},{13,9},{2,14},{6,2},{... | collective-permute-start | bytes 786440 | tf_op jit(solution)/shard_map/ppermute | solution.py:393
  44.8 21.0 %collective-permute-start.6 = (f32[2,256,128]{2,1,0:T(8,128)S(1)}, f32[2,256,128]{2,1,0:T(8,128)S(1)}, u32[]{:S(2)}, u32[]{:S(2)}) collective-permute-start(f32[2,256,128]{2,1,0:T(8,128)S(1)} %slice_bitcast_fusion.5), channel_id=1, source_target_pairs={{0,4},{4,8},{8,12},{12,0},{1,5},{5,9},{9,13},{13,1},{2,6},{6,10},{... | collective-permute-start | bytes 786440 | tf_op jit(solution)/shard_map/ppermute | solution.py:392
  44.8 1.6 copy-start.13
  46.4 1.6 copy-start.14
  52.9 30.2 %collective-permute-start.11 = (f32[2,256,128]{2,1,0:T(8,128)S(1)}, f32[2,256,128]{2,1,0:T(8,128)S(1)}, u32[]{:S(2)}, u32[]{:S(2)}) collective-permute-start(f32[2,256,128]{2,1,0:T(8,128)S(1)} %slice_bitcast_fusion.2), channel_id=1, source_target_pairs={{0,12},{4,0},{8,4},{12,8},{1,13},{5,1},{9,5},{13,9},{2,14},{6,2},{... | collective-permute-start | bytes 786440 | tf_op jit(solution)/shard_map/ppermute | solution.py:393
  63.0 20.1 %collective-permute-start.10 = (f32[2,256,128]{2,1,0:T(8,128)S(1)}, f32[2,256,128]{2,1,0:T(8,128)S(1)}, u32[]{:S(2)}, u32[]{:S(2)}) collective-permute-start(f32[2,256,128]{2,1,0:T(8,128)S(1)} %slice_bitcast_fusion.3), channel_id=1, source_target_pairs={{0,4},{4,8},{8,12},{12,0},{1,5},{5,9},{9,13},{13,1},{2,6},{6,10},{... | collective-permute-start | bytes 786440 | tf_op jit(solution)/shard_map/ppermute | solution.py:392
  63.1 16.4 %collective-permute-start.9 = (f32[2,2,256,128]{3,2,1,0:T(8,128)}, f32[2,2,256,128]{3,2,1,0:T(8,128)S(1)}, u32[]{:S(2)}, u32[]{:S(2)}) collective-permute-start(f32[2,2,256,128]{3,2,1,0:T(8,128)} %collective-permute-done.5.refs_2_.refs_5_), channel_id=1, source_target_pairs={{0,12},{4,0},{8,4},{12,8},{1,13},{5,1},{9,5},{13,9},{2,14},{6,2},{... | collective-permute-start | bytes 1572872 | tf_op jit(solution)/shard_map/ppermute | solution.py:393
  65.8 4.1 %copy-start.6 = (f32[2,256,128]{2,1,0:T(8,128)}, f32[2,256,128]{2,1,0:T(8,128)S(1)}, u32[]{:S(2)}) copy-start(f32[2,256,128]{2,1,0:T(8,128)S(1)} %collective-permute-done.7.refs_4_.refs_9_) | copy-start | bytes 786436
  65.8 17.2 %collective-permute-start.8 = (f32[2,2,256,128]{3,2,1,0:T(8,128)}, f32[2,2,256,128]{3,2,1,0:T(8,128)S(1)}, u32[]{:S(2)}, u32[]{:S(2)}) collective-permute-start(f32[2,2,256,128]{3,2,1,0:T(8,128)} %collective-permute-done.5.refs_2_.refs_5_), channel_id=1, source_target_pairs={{0,4},{4,8},{8,12},{12,0},{1,5},{5,9},{9,13},{13,1},{2,6},{6,10},{... | collective-permute-start | bytes 1572872 | tf_op jit(solution)/shard_map/ppermute | solution.py:392
  65.8 4.1 %copy-start.7 = (f32[2,256,128]{2,1,0:T(8,128)}, f32[2,256,128]{2,1,0:T(8,128)S(1)}, u32[]{:S(2)}) copy-start(f32[2,256,128]{2,1,0:T(8,128)S(1)} %collective-permute-done.6.refs_3_.refs_8_) | copy-start | bytes 786436
  79.5 7.6 %copy-start.3 = (f32[2,2,256,128]{3,2,1,0:T(8,128)}, f32[2,2,256,128]{3,2,1,0:T(8,128)S(1)}, u32[]{:S(2)}) copy-start(f32[2,2,256,128]{3,2,1,0:T(8,128)S(1)} %collective-permute-done.9.refs_1_.refs_7_) | copy-start | bytes 1572868
  79.5 12.5 %collective-permute-start.13 = (f32[2,256,128]{2,1,0:T(8,128)S(1)}, f32[2,256,128]{2,1,0:T(8,128)S(1)}, u32[]{:S(2)}, u32[]{:S(2)}) collective-permute-start(f32[2,256,128]{2,1,0:T(8,128)S(1)} %slice_bitcast_fusion), channel_id=1, source_target_pairs={{0,12},{4,0},{8,4},{12,8},{1,13},{5,1},{9,5},{13,9},{2,14},{6,2},{... | collective-permute-start | bytes 786440 | tf_op jit(solution)/shard_map/ppermute | solution.py:393
  83.0 4.1 %copy-start.4 = (f32[2,2,256,128]{3,2,1,0:T(8,128)}, f32[2,2,256,128]{3,2,1,0:T(8,128)S(1)}, u32[]{:S(2)}) copy-start(f32[2,2,256,128]{3,2,1,0:T(8,128)S(1)} %collective-permute-done.8.refs_0_.refs_6_) | copy-start | bytes 1572868
  83.0 12.7 %collective-permute-start.12 = (f32[2,256,128]{2,1,0:T(8,128)S(1)}, f32[2,256,128]{2,1,0:T(8,128)S(1)}, u32[]{:S(2)}, u32[]{:S(2)}) collective-permute-start(f32[2,256,128]{2,1,0:T(8,128)S(1)} %slice_bitcast_fusion.1), channel_id=1, source_target_pairs={{0,4},{4,8},{8,12},{12,0},{1,5},{5,9},{9,13},{13,1},{2,6},{6,10},{... | collective-permute-start | bytes 786440 | tf_op jit(solution)/shard_map/ppermute | solution.py:392
  83.1 4.0 %copy-start.8 = (f32[2,256,128]{2,1,0:T(8,128)}, f32[2,256,128]{2,1,0:T(8,128)S(1)}, u32[]{:S(2)}) copy-start(f32[2,256,128]{2,1,0:T(8,128)S(1)} %collective-permute-done.11.refs_3_.refs_11_) | copy-start | bytes 786436
  83.1 3.9 %copy-start.9 = (f32[2,256,128]{2,1,0:T(8,128)}, f32[2,256,128]{2,1,0:T(8,128)S(1)}, u32[]{:S(2)}) copy-start(f32[2,256,128]{2,1,0:T(8,128)S(1)} %collective-permute-done.10.refs_2_.refs_10_) | copy-start | bytes 786436
  87.1 12.0 %copy-start.15 = (f32[16,256,128]{2,1,0:T(8,128)}, f32[16,256,128]{2,1,0:T(8,128)S(1)}, u32[]{:S(2)}) copy-start(f32[16,256,128]{2,1,0:T(8,128)S(1)} %get-tuple-element.71.stat_ref) | copy-start | bytes 6291460
  92.0 7.1 %copy-start.10 = (f32[2,256,128]{2,1,0:T(8,128)}, f32[2,256,128]{2,1,0:T(8,128)S(1)}, u32[]{:S(2)}) copy-start(f32[2,256,128]{2,1,0:T(8,128)S(1)} %collective-permute-done.13.refs_1_.refs_13_) | copy-start | bytes 786436
  95.7 3.4 %copy-start.11 = (f32[2,256,128]{2,1,0:T(8,128)}, f32[2,256,128]{2,1,0:T(8,128)S(1)}, u32[]{:S(2)}) copy-start(f32[2,256,128]{2,1,0:T(8,128)S(1)} %collective-permute-done.12.refs_0_.refs_12_) | copy-start | bytes 786436
  99.1 1.3 copy-start.16
  100.4 6.8 %copy-start.12 = (f32[8,256]{1,0:T(8,128)}, f32[8,256]{1,0:T(8,128)S(1)}, u32[]{:S(2)}) copy-start(f32[8,256]{1,0:T(8,128)S(1)} %get-tuple-element.77.sq0_ref) | copy-start | bytes 24580
  100.4 3.7 %collective-permute-start.16 = (f32[8,256]{1,0:T(8,128)S(1)}, f32[8,256]{1,0:T(8,128)S(1)}, u32[]{:S(2)}, u32[]{:S(2)}) collective-permute-start(f32[8,256]{1,0:T(8,128)S(1)} %get-tuple-element.77.sq0_ref), channel_id=1, source_target_pairs={{0,3},{1,0},{2,1},{3,2},{4,7},{5,4},{6,5},{7,6},{8,11},{9,8},{10,9... | collective-permute-start | bytes 24584 | tf_op jit(solution)/shard_map/ppermute | solution.py:460
  102.9 4.0 %collective-permute-start.15 = (f32[8,256]{1,0:T(8,128)S(1)}, f32[8,256]{1,0:T(8,128)S(1)}, u32[]{:S(2)}, u32[]{:S(2)}) collective-permute-start(f32[8,256]{1,0:T(8,128)S(1)} %get-tuple-element.77.sq0_ref), channel_id=1, source_target_pairs={{0,2},{1,3},{2,0},{3,1},{4,6},{5,7},{6,4},{7,5},{8,10},{9,11},{10,... | collective-permute-start | bytes 24584 | tf_op jit(solution)/shard_map/ppermute | solution.py:460
  103.5 3.7 %collective-permute-start.14 = (f32[8,256]{1,0:T(8,128)S(1)}, f32[8,256]{1,0:T(8,128)S(1)}, u32[]{:S(2)}, u32[]{:S(2)}) collective-permute-start(f32[8,256]{1,0:T(8,128)S(1)} %get-tuple-element.77.sq0_ref), channel_id=1, source_target_pairs={{0,1},{1,2},{2,3},{3,0},{4,5},{5,6},{6,7},{7,4},{8,9},{9,10},{10,1... | collective-permute-start | bytes 24584 | tf_op jit(solution)/shard_map/ppermute | solution.py:460
  104.1 3.1 %copy-start.19 = (f32[8,256]{1,0:T(8,128)}, f32[8,256]{1,0:T(8,128)S(1)}, u32[]{:S(2)}) copy-start(f32[8,256]{1,0:T(8,128)S(1)} %collective-permute-done.16.sq3_ref) | copy-start | bytes 24580
  107.0 0.6 copy-start.20
  107.2 0.6 copy-start.21
  124.2 35.7 %all-to-all-start = ((f32[32,64,128]{2,1,0:T(8,128)}), f32[32,64,128]{2,1,0:T(8,128)S(1)}, u32[]{:S(2)}, u32[]{:S(2)}) async-start(f32[32,64,128]{2,1,0:T(8,128)} %bitcast.63), calls=%async_computation | async-start | bytes 2097152 | tf_op jit(solution)/shard_map/all_to_all | solution.py:488
  160.0 19.0 %copy-start.18 = (f32[16,256,128]{2,1,0:T(8,128)S(1)}, f32[16,256,128]{2,1,0:T(8,128)}, u32[]{:S(2)}) copy-start(f32[16,256,128]{2,1,0:T(8,128)} %get-tuple-element.78) | copy-start | bytes 6291460
  174.5 22.4 %all-to-all-start.2 = ((f32[32,72,128]{2,1,0:T(8,128)}), f32[32,72,128]{2,1,0:T(8,128)S(1)}, u32[]{:S(2)}, u32[]{:S(2)}) async-start(f32[32,72,128]{2,1,0:T(8,128)} %broadcast_in_dim.15), calls=%async_computation.2 | async-start | bytes 2359296 | tf_op jit(solution)/shard_map/all_to_all | solution.py:507
Sparse Core Ops, SparseCore 0:
  42.1 52.6 all-gather.4
  124.4 57.2 all-gather.6

commit v3 on v2

--- a/solution.py
+++ b/solution.py
@@ -23,7 +23,7 @@
 STEP = 4
 EARLY = 4
 WIDE = 8
-TILE = 2
+TILE = 1
 N_CTX = 16
 SROWS = WID + 8
 
@@ -56,7 +56,7 @@
     return e / row_sum(e)
 
 
-SOURCES = ((0, 3), (0, 1), (1, 0), (1, 3), (1, 1), (2, 0), (0, 2), (2, 3), (2, 1), (1, 2), (2, 2))
+SOURCES = ((0, 3), (0, 1), (1, 0), (0, 2), (1, 3), (1, 1), (2, 0), (2, 3), (2, 1), (1, 2), (2, 2))
 
 
 def bounds(docs):
@@ -165,7 +165,7 @@
         acc[here, :] = acc0_ref[some].reshape(rows, WID)
         return carry
 
-    lax.fori_loop(0, tiles, take_up, 0)
+    lax.fori_loop(0, tiles, take_up, 0, unroll=True)
 
     @pl.when(g == 0)
     def _():
@@ -220,7 +220,7 @@
             stat_out[some] = jnp.where(lane == 0, m_sc[here, :], stat).reshape(TILE, TOK, WID)
             return carry
 
-        lax.fori_loop(0, tiles, put_down, 0)
+        lax.fori_loop(0, tiles, put_down, 0, unroll=True)
         return
     total = jnp.zeros((TOK, WID), F32)
     for i in range(tiles):
@@ -303,7 +303,7 @@
 
 def key_map_kernel(docs, k_ref, kf_ref, gkf_ref, s_ref, wk_ref, *refs):
     pieces, (mk_ref, flags, order, buf, sem) = refs[:-5], refs[-5:]
-    note_wanted(docs, flags, (0, 1, 2, 3, 4, 5, 7, 8, 6, 9, 10))
+    note_wanted(docs, flags, (0, 1, 2, 4, 5, 6, 7, 8, 3, 9, 10))
     state = [split(s_ref[h, :WID]) for h in range(KVH)]
     norm = [s_ref[h, WID : WID + 1] for h in range(KVH)]
     wk = [split(wk_ref[h]) for h in range(KVH)]
@@ -419,9 +419,12 @@
     arrived = down(mine), right(mine), left(mine)
     held = local(0, ())
     (za, yp0, ym0), held = lax.optimization_barrier((arrived, held))
+    cross = lambda p, m: (right(p[0]), left(m[1]))
     zb, yp1, ym1 = down(za), right(za), left(za)
+    across = [cross(yp0, ym0)]
     yp2, ym2 = right(zb), left(zb)
-    across = [(right(p[0]), left(m[1])) for p, m in ((yp0, ym0), (yp1, ym1), (yp2, ym2))]
+    across.append(cross(yp1, ym1))
+    across.append(cross(yp2, ym2))
 
     qf, num, acc, stat, a, kf, states = local(1, held)
     block_states = lax.all_gather(states, CTX)
@@ -453,9 +456,8 @@
             name="attend",
         )(docs, q, acc, stat, *whole, *[x for pair in halves for x in pair])
 
-    acc, stat = attend(acc, stat, [yp0, ym0, za], [], 0, False, 14)
-    acc, stat = attend(acc, stat, [yp1, ym1, zb], [across[0]], 3, False, 16)
-    acc, stat = attend(acc, stat, [yp2, ym2], [across[1]], 7, False, 12)
+    acc, stat = attend(acc, stat, [yp0, ym0, za], [across[0]], 0, False, 16)
+    acc, stat = attend(acc, stat, [yp1, ym1, zb, yp2, ym2], [across[1]], 4, False, 22)
     teacher, squares = attend(acc, stat, [], [across[2]], 10, True, 6)
     others = [lax.ppermute(squares, "head", [(i, (i + k) % 4) for i in range(4)]) for k in (1, 2, 3)]
 

time: 215 us -> 224 us (1.042)
  starting transfers between devices: 59 us -> 72.5 us
  Pallas kernels: 54.8 us -> 49.3 us
    ppermute x6, waiting for transfers between devices: 14.5 us -> 0.32 us  [body(): lax.ppermute(x, 'ctx_1', [(i, (i - 1) % 4) for i in range(4)])]
    ppermute x6, waiting for transfers between devices: 3.77 us -> 17.9 us  [body(): lax.ppermute(x, 'ctx_1', [(i, (i + 1) % 4) for i in range(4)])]
    all_to_all x1, starting transfers between devices: 17.2 us -> 30.4 us  [body(): lax.all_to_all(x.reshape(32, -1, WID), DP_CTX, 0, 0, tiled=True)]
    pallas_call x4 -> x3, Pallas kernels: 15.2 us -> 9.67 us  [attend(): pl.pallas_call(functools.partial(attend_kernel, len(whole), len(halves),...]
    ppermute x6, starting transfers between devices: 0.16 us -> 2.43 us  [body(): lax.ppermute(x, 'ctx_1', [(i, (i + 1) % 4) for i in range(4)])]
    unnamed x48 -> x46, local copies, waits for them, and re-layouts: 13.3 us -> 13.3 us
  transfers between devices with their start and end apart: 21 -> 21, of which waited for: 7 -> 9; matrix products, arithmetic and copies ran while one was open for 4% -> 5% of each run, Pallas kernels for 16% -> 13%
where the time goes in v3:
time: 224 us; the launch traced here: 223 us
  starting transfers between devices  72.5 us (32%)
  waiting for transfers between devices  51.6 us (23%)
  Pallas kernels  49.3 us (22%)
  local copies, waits for them, and re-layouts  21.6 us (10%)
  between operations  14.4 us (6%)
  blocking collectives  13.4 us (6%)
    all_to_all x1, starting transfers between devices, body(): lax.all_to_all(x.reshape(32, -1, WID), DP_CTX, 0, 0, tiled=True)  30.4 us
    ppermute x6, starting transfers between devices, body(): lax.ppermute(x, 'ctx_1', [(i, (i - 1) % 4) for i in range(4)])  22.1 us
    ppermute x6, waiting for transfers between devices, body(): lax.ppermute(x, 'ctx_1', [(i, (i + 1) % 4) for i in range(4)])  17.9 us
    pallas_call x1, Pallas kernels, body(): pl.pallas_call(student_kernel, grid_spec=pltpu.PrefetchScalarGridSpec(num...  16.4 us
    all_to_all x1, waiting for transfers between devices, body(): lax.all_to_all(jnp.broadcast_to(parts, (32, *parts.shape)), DP_CTX, 0, 0,...  15.4 us
    pallas_call x2, Pallas kernels, local(): pl.pallas_call(local_kernel, grid=(GRP // EARLY,), in_specs=[part(TOK, WI...  15.3 us
    all_to_all x1, waiting for transfers between devices, body(): lax.all_to_all(x.reshape(32, -1, WID), DP_CTX, 0, 0, tiled=True)  14.9 us
    all_to_all x1, blocking collectives, body(): lax.all_to_all(x.reshape(32, -1, WID), DP_CTX, 0, 0, tiled=True)  13.4 us
  transfers between devices with their start and end apart: 21, of which 9 were waited for; matrix products, arithmetic and copies ran while one was open for 5% of the time, Pallas kernels for 13%

profile of v3, /device:TPU:1, one launch (start us, length us, event | category | flops | bytes accessed | tf_op | source)
XLA Modules:
  0.0 222.9 jit_solution(14711839281071948075)
XLA Ops:
  7.2 2.0 copy_bitcast_fusion.1
  9.3 3.6 %collective-permute-start.2 = (f32[2,2,256,128]{3,2,1,0:T(8,128)S(1)}, f32[2,2,256,128]{3,2,1,0:T(8,128)S(1)}, u32[]{:S(2)}, u32[]{:S(2)}) collective-permute-start(f32[2,2,256,128]{3,2,1,0:T(8,128)S(1)} %pad_maximum_fusion), channel_id=1, source_target_pairs={{0,12},{4,0},{8,4},{12,8},{1,13},{5,1},{9,5},{13,9},{2,14},{6,2},{... | collective-permute-start | bytes 1572872 | tf_op jit(solution)/shard_map/ppermute | solution.py:393
  12.9 4.3 %collective-permute-start = (f32[2,2,256,128]{3,2,1,0:T(8,128)S(1)}, f32[2,2,256,128]{3,2,1,0:T(8,128)}, u32[]{:S(2)}, u32[]{:S(2)}) collective-permute-start(f32[2,2,256,128]{3,2,1,0:T(8,128)S(1)} %pad_maximum_fusion), channel_id=1, source_target_pairs={{0,16},{16,32},{32,48},{1,17},{17,33},{33,49},{2,18},{18,34},{34,5... | collective-permute-start | bytes 1572872 | tf_op jit(solution)/shard_map/ppermute | solution.py:391
  17.3 2.0 copy.35
  19.2 7.6 %local.2 = (f32[16,256,128]{2,1,0:T(8,128)}, f32[16,256,128]{2,1,0:T(8,128)}, f32[16,256,128]{2,1,0:T(8,128)}, f32[16,256,128]{2,1,0:T(8,128)}, f32[16,256,256]{...) custom-call(f32[16,256,128]{2,1,0:T(8,128)} %bitcast.47, f32[2,256,128]{2,1,0:T(8,128)} %get-tuple-element.97.k_ref, ...), custom_call_target="tpu_custom_call" | custom-call | flops 8000000000 | bytes 2400000 | tf_op jit(solution)/shard_map/local/pallas_call | solution.py:405
  26.8 4.9 %collective-permute-start.7 = (f32[2,2,256,128]{3,2,1,0:T(8,128)}, f32[2,2,256,128]{3,2,1,0:T(8,128)}, u32[]{:S(2)}, u32[]{:S(2)}) collective-permute-start(f32[2,2,256,128]{3,2,1,0:T(8,128)} %collective-permute-done.refs_2_), channel_id=1, source_target_pairs={{0,16},{16,32},{32,48},{1,17},{17,33},{33,49},{2,18},{18,34},{34,5... | collective-permute-start | bytes 1572872 | tf_op jit(solution)/shard_map/ppermute | solution.py:391
  31.8 2.4 %collective-permute-start.6 = (f32[2,2,256,128]{3,2,1,0:T(8,128)}, f32[2,2,256,128]{3,2,1,0:T(8,128)}, u32[]{:S(2)}, u32[]{:S(2)}) collective-permute-start(f32[2,2,256,128]{3,2,1,0:T(8,128)} %collective-permute-done.refs_2_), channel_id=1, source_target_pairs={{0,12},{4,0},{8,4},{12,8},{1,13},{5,1},{9,5},{13,9},{2,14},{6,2},{... | collective-permute-start | bytes 1572872 | tf_op jit(solution)/shard_map/ppermute | solution.py:393
  34.2 0.7 slice_bitcast_fusion.5
  34.9 0.7 slice_bitcast_fusion.4
  35.6 2.7 %collective-permute-start.4 = (f32[2,256,128]{2,1,0:T(8,128)}, f32[2,256,128]{2,1,0:T(8,128)S(1)}, u32[]{:S(2)}, u32[]{:S(2)}) collective-permute-start(f32[2,256,128]{2,1,0:T(8,128)} %slice_bitcast_fusion.4), channel_id=1, source_target_pairs={{0,12},{4,0},{8,4},{12,8},{1,13},{5,1},{9,5},{13,9},{2,14},{6,2},{... | collective-permute-start | bytes 786440 | tf_op jit(solution)/shard_map/ppermute | solution.py:393
  38.3 7.7 %local.3 = (f32[16,256,128]{2,1,0:T(8,128)}, f32[16,256,128]{2,1,0:T(8,128)}, f32[16,256,128]{2,1,0:T(8,128)}, f32[16,256,128]{2,1,0:T(8,128)}, f32[16,256,256]{...) custom-call(f32[16,256,128]{2,1,0:T(8,128)} %bitcast.48, ...), custom_call_target="tpu_custom_call", output_to_operand_aliasing={{0}: (5, {}), {1}: (6, {}), {2}: (7, {}), {3}: (8, {}), {4}... | custom-call | flops 8000000000 | bytes 2400000 | tf_op jit(solution)/shard_map/local/pallas_call | solution.py:405
  46.1 2.7 %collective-permute-start.9 = (f32[2,2,256,128]{3,2,1,0:T(8,128)}, f32[2,2,256,128]{3,2,1,0:T(8,128)S(1)}, u32[]{:S(2)}, u32[]{:S(2)}) collective-permute-start(f32[2,2,256,128]{3,2,1,0:T(8,128)} %collective-permute-done.7.refs_2_.refs_5_), channel_id=1, source_target_pairs={{0,12},{4,0},{8,4},{12,8},{1,13},{5,1},{9,5},{13,9},{2,14},{6,2},{... | collective-permute-start | bytes 1572872 | tf_op jit(solution)/shard_map/ppermute | solution.py:393
  48.8 0.3 collective-permute-done.4.refs_4_.refs_9_
  49.1 3.0 %collective-permute-done.3.refs_3_.refs_8_ = f32[2,256,128]{2,1,0:T(8,128)} collective-permute-done((f32[2,256,128]{2,1,0:T(8,128)}, f32[2,256,128]{2,1,0:T(8,128)}, u32[]{:S(2)}, u32[]{:S(2)}) %collective-permute-start.3) | collective-permute-done | bytes 262176 | tf_op jit(solution)/shard_map/ppermute | solution.py:392
  52.2 1.6 copy-done.12
  53.7 1.6 copy-done.13
  55.3 3.2 %attend.3 = (f32[16,256,128]{2,1,0:T(8,128)S(1)}, f32[16,256,128]{2,1,0:T(8,128)S(1)}) custom-call(s32[16]{0:T(128)S(1)} %bitcast.56, f32[16,256,128]{2,1,0:T(8,128)S(1)} %bitcast.50, f32[16,256,128]{2,1,0:T(8,128)S(1)} %copy-done.12, f32[16,256,128]{2,1,0:T(8,128)S(1)} %copy-done.13, f32[2,2,256,128]{3,2,1,0:T(8,128)S(1)} %collective-permute-done.1.refs_0_, ...), custom_call_target="tpu_custom_call" | custom-call | flops 16000000000 | bytes 4800000 | tf_op jit(solution)/shard_map/attend/pallas_call | solution.py:436
  58.6 2.3 %collective-permute-start.8 = (f32[2,2,256,128]{3,2,1,0:T(8,128)}, f32[2,2,256,128]{3,2,1,0:T(8,128)S(1)}, u32[]{:S(2)}, u32[]{:S(2)}) collective-permute-start(f32[2,2,256,128]{3,2,1,0:T(8,128)} %collective-permute-done.7.refs_2_.refs_5_), channel_id=1, source_target_pairs={{0,4},{4,8},{8,12},{12,0},{1,5},{5,9},{9,13},{13,1},{2,6},{6,10},{... | collective-permute-start | bytes 1572872 | tf_op jit(solution)/shard_map/ppermute | solution.py:392
  60.8 1.0 slice_bitcast_fusion.2
  61.8 8.0 %collective-permute-start.11 = (f32[2,256,128]{2,1,0:T(8,128)S(1)}, f32[2,256,128]{2,1,0:T(8,128)S(1)}, u32[]{:S(2)}, u32[]{:S(2)}) collective-permute-start(f32[2,256,128]{2,1,0:T(8,128)S(1)} %slice_bitcast_fusion.2), channel_id=1, source_target_pairs={{0,12},{4,0},{8,4},{12,8},{1,13},{5,1},{9,5},{13,9},{2,14},{6,2},{... | collective-permute-start | bytes 786440 | tf_op jit(solution)/shard_map/ppermute | solution.py:393
  69.8 1.0 slice_bitcast_fusion.3
  70.9 2.7 %collective-permute-start.13 = (f32[2,256,128]{2,1,0:T(8,128)S(1)}, f32[2,256,128]{2,1,0:T(8,128)S(1)}, u32[]{:S(2)}, u32[]{:S(2)}) collective-permute-start(f32[2,256,128]{2,1,0:T(8,128)S(1)} %slice_bitcast_fusion), channel_id=1, source_target_pairs={{0,12},{4,0},{8,4},{12,8},{1,13},{5,1},{9,5},{13,9},{2,14},{6,2},{... | collective-permute-start | bytes 786440 | tf_op jit(solution)/shard_map/ppermute | solution.py:393
  73.6 3.2 %collective-permute-done.8.refs_3_.refs_6_ = f32[2,2,256,128]{3,2,1,0:T(8,128)S(1)} collective-permute-done((f32[2,2,256,128]{3,2,1,0:T(8,128)}, f32[2,2,256,128]{3,2,1,0:T(8,128)S(1)}, u32[]{:S(2)}, u32[]{:S(2)}) %collective-permute-start.8) | collective-permute-done | bytes 524320 | tf_op jit(solution)/shard_map/ppermute | solution.py:392
  77.0 5.5 %collective-permute-done.10.refs_5_.refs_10_ = f32[2,256,128]{2,1,0:T(8,128)S(1)} collective-permute-done((f32[2,256,128]{2,1,0:T(8,128)S(1)}, f32[2,256,128]{2,1,0:T(8,128)S(1)}, u32[]{:S(2)}, u32[]{:S(2)}) %collective-permute-start.10) | collective-permute-done | bytes 262176 | tf_op jit(solution)/shard_map/ppermute | solution.py:392
  82.5 3.5 %attend.4 = (f32[16,256,128]{2,1,0:T(8,128)S(1)}, f32[16,256,128]{2,1,0:T(8,128)S(1)}) custom-call(s32[16]{0:T(128)S(1)} %bitcast.57, f32[16,256,128]{2,1,0:T(8,128)S(1)} %bitcast.51, f32[16,256,128]{2,1,0:T(8,128)S(1)} %get-tuple-element.65.acc0_ref, f32[16,256,128]{2,1,0:T(8,128)S(1)} %get-tuple-element.66.stat_ref, ...), custom_call_target="tpu_custom_call" | custom-call | flops 22000001024 | bytes 6600000 | tf_op jit(solution)/shard_map/attend/pallas_call | solution.py:436
  86.1 6.2 %collective-permute-done.12.refs_0_.refs_12_ = f32[2,256,128]{2,1,0:T(8,128)S(1)} collective-permute-done((f32[2,256,128]{2,1,0:T(8,128)S(1)}, f32[2,256,128]{2,1,0:T(8,128)S(1)}, u32[]{:S(2)}, u32[]{:S(2)}) %collective-permute-start.12) | collective-permute-done | bytes 262176 | tf_op jit(solution)/shard_map/ppermute | solution.py:392
  92.3 2.9 %attend.5 = (f32[16,256,128]{2,1,0:T(8,128)S(1)}, f32[8,256]{1,0:T(8,128)S(1)}) custom-call(s32[16]{0:T(128)S(1)} %bitcast.58, f32[16,256,128]{2,1,0:T(8,128)S(1)} %bitcast.52, f32[16,256,128]{2,1,0:T(8,128)S(1)} %get-tuple-element.69.acc0_ref, f32[16,256,128]{2,1,0:T(8,128)S(1)} %get-tuple-element.67.stat_ref, ...), custom_call_target="tpu_custom_call" | custom-call | flops 6000000000 | bytes 1800000 | tf_op jit(solution)/shard_map/attend/pallas_call | solution.py:436
  95.2 1.3 copy-done.15
  96.5 2.5 %collective-permute-start.16 = (f32[8,256]{1,0:T(8,128)S(1)}, f32[8,256]{1,0:T(8,128)S(1)}, u32[]{:S(2)}, u32[]{:S(2)}) collective-permute-start(f32[8,256]{1,0:T(8,128)S(1)} %get-tuple-element.73.sq0_ref), channel_id=1, source_target_pairs={{0,3},{1,0},{2,1},{3,2},{4,7},{5,4},{6,5},{7,6},{8,11},{9,8},{10,9... | collective-permute-start | bytes 24584 | tf_op jit(solution)/shard_map/ppermute | solution.py:462
  99.1 0.5 collective-permute-start.15
  99.5 0.6 collective-permute-start.14
  100.2 2.9 %collective-permute-done.15.sq2_ref = f32[8,256]{1,0:T(8,128)S(1)} collective-permute-done((f32[8,256]{1,0:T(8,128)S(1)}, f32[8,256]{1,0:T(8,128)S(1)}, u32[]{:S(2)}, u32[]{:S(2)}) %collective-permute-start.15) | collective-permute-done | bytes 8224 | tf_op jit(solution)/shard_map/ppermute | solution.py:462
  103.3 0.4 copy-done.19
  103.7 0.2 copy-done.20
  103.9 16.4 %student.1 = (f32[16,256,128]{2,1,0:T(8,128)}, f32[16,128,128]{2,1,0:T(8,128)}, f32[2,256,128]{2,1,0:T(8,128)}, f32[2,256,128]{2,1,0:T(8,128)}, f32[2,136,128]{2,1,0:T(8,128)}) custom-call(s32[16]{0:T(128)} %bitcast.53, f32[16,256,128]{2,1,0:T(8,128)} %bitcast.49, f32[16,256,128]{2,1,0:T(8,128)} %get-tuple-element.58.qf_ref, ...), custom_call_target="tpu_custom_call" | custom-call | flops 24999999488 | bytes 7500000 | tf_op jit(solution)/shard_map/student/pallas_call | solution.py:464
  120.3 30.4 %all-to-all-start = ((f32[32,64,128]{2,1,0:T(8,128)}), f32[32,64,128]{2,1,0:T(8,128)S(1)}, u32[]{:S(2)}, u32[]{:S(2)}) async-start(f32[32,64,128]{2,1,0:T(8,128)} %bitcast.61), calls=%async_computation | async-start | bytes 2097152 | tf_op jit(solution)/shard_map/all_to_all | solution.py:490
  150.8 3.5 %key_map.1 = f32[2,128,128]{2,1,0:T(8,128)} custom-call(s32[16]{0:T(128)} %bitcast.54, f32[2,256,128]{2,1,0:T(8,128)} %get-tuple-element.97.k_ref, f32[2,256,128]{2,1,0:T(8,128)} %get-tuple-element.71.kf_ref, f32[2,256,128]{2,1,0:T(8,128)} %get-tuple-element.76.gkf_ref, f32[2,136,128]{2,1,0:T(8,128)} %get-tuple-element.75.s_ref, f32[2,128,128]{2,1,0:T(8,128)} %wk_ref.7, ...), custom_call_target="tpu_custom_call" | custom-call | flops 10000000000 | bytes 3000000 | tf_op jit(solution)/shard_map/key_map/pallas_call | solution.py:492
  154.3 14.9 %all-to-all-done = f32[32,64,128]{2,1,0:T(8,128)S(1)} async-done(((f32[32,64,128]{2,1,0:T(8,128)}), f32[32,64,128]{2,1,0:T(8,128)S(1)}, u32[]{:S(2)}, u32[]{:S(2)}) %all-to-all-start) | async-done | bytes 1048608 | tf_op jit(solution)/shard_map/all_to_all | solution.py:490
  169.3 13.4 %all_to_all.15 = f32[32,8,128]{2,1,0:T(8,128)S(1)} all-to-all(f32[32,8,128]{2,1,0:T(8,128)} %bitcast.66), channel_id=1, replica_groups=mesh['dp'=2,'ctx_0'=4,'ctx_1'=4,'head'=4] {'dp','ctx_0','ctx_1'}, dimensions={0} | all-to-all | bytes 262144 | tf_op jit(solution)/shard_map/all_to_all | solution.py:490
  182.7 1.1 broadcast_in_dim.15
  183.8 4.5 %all-to-all-start.2 = ((f32[32,72,128]{2,1,0:T(8,128)}), f32[32,72,128]{2,1,0:T(8,128)S(1)}, u32[]{:S(2)}, u32[]{:S(2)}) async-start(f32[32,72,128]{2,1,0:T(8,128)} %broadcast_in_dim.15), calls=%async_computation.2 | async-start | bytes 2359296 | tf_op jit(solution)/shard_map/all_to_all | solution.py:509
  188.3 2.5 %copy.27 = f32[1,256,16,128]{3,2,1,0:T(8,128)} copy(f32[1,256,16,128]{3,1,2,0:T(8,128)S(1)} %bitcast.60) | data formatting | bytes 4194304
  190.8 15.4 %all-to-all-done.2 = f32[32,72,128]{2,1,0:T(8,128)S(1)} async-done(((f32[32,72,128]{2,1,0:T(8,128)}), f32[32,72,128]{2,1,0:T(8,128)S(1)}, u32[]{:S(2)}, u32[]{:S(2)}) %all-to-all-start.2) | async-done | bytes 1179680 | tf_op jit(solution)/shard_map/all_to_all | solution.py:509
  206.2 0.7 slice.37
  206.9 1.1 slice.36
  208.0 4.4 %later.1 = (f32[2,256,128]{2,1,0:T(8,128)}, f32[2,256,128]{2,1,0:T(8,128)}) custom-call(s32[16]{0:T(128)} %bitcast.55, f32[16,2,136,128]{3,2,1,0:T(8,128)} %bitcast.59, f32[2,256,128]{2,1,0:T(8,128)} %get-tuple-element.76.gkf_ref, f32[2,256,128]{2,1,0:T(8,128)} %get-tuple-element.77.gv_ref, f32[2,256,128]{2,1,0:T(8,128)} %get-tuple-element.71.kf_ref, ...), custom_call_target="tpu_custom_call" | custom-call | tf_op jit(solution)/shard_map/later/pallas_call | solution.py:511
  212.4 1.9 copy.28
  214.2 1.9 copy.29
  (65 shorter events, 0.7 us)
Async XLA Ops:
  7.2 10.1 %copy-start.16 = (f32[1,256,16,128]{3,2,1,0:T(8,128)S(1)}, f32[1,256,16,128]{3,2,1,0:T(8,128)}, u32[]{:S(2)}) copy-start(f32[1,256,16,128]{3,2,1,0:T(8,128)} %param.6) | copy-start | bytes 6291460
  7.2 96.1 %all-gather.5.cloned.1.call-start = ((), (), s32[]{:S(2)}) async-start(), calls=%async_computation.3 | async-start | bytes 2367488 | tf_op jit(solution)/shard_map/all_gather | solution.py:430
  9.3 17.5 %collective-permute-start.2 = (f32[2,2,256,128]{3,2,1,0:T(8,128)S(1)}, f32[2,2,256,128]{3,2,1,0:T(8,128)S(1)}, u32[]{:S(2)}, u32[]{:S(2)}) collective-permute-start(f32[2,2,256,128]{3,2,1,0:T(8,128)S(1)} %pad_maximum_fusion), channel_id=1, source_target_pairs={{0,12},{4,0},{8,4},{12,8},{1,13},{5,1},{9,5},{13,9},{2,14},{6,2},{... | collective-permute-start | bytes 1572872 | tf_op jit(solution)/shard_map/ppermute | solution.py:393
  12.9 13.9 %collective-permute-start.1 = (f32[2,2,256,128]{3,2,1,0:T(8,128)S(1)}, f32[2,2,256,128]{3,2,1,0:T(8,128)S(1)}, u32[]{:S(2)}, u32[]{:S(2)}) collective-permute-start(f32[2,2,256,128]{3,2,1,0:T(8,128)S(1)} %pad_maximum_fusion), channel_id=1, source_target_pairs={{0,4},{4,8},{8,12},{12,0},{1,5},{5,9},{9,13},{13,1},{2,6},{6,10},{... | collective-permute-start | bytes 1572872 | tf_op jit(solution)/shard_map/ppermute | solution.py:392
  12.9 13.9 %collective-permute-start = (f32[2,2,256,128]{3,2,1,0:T(8,128)S(1)}, f32[2,2,256,128]{3,2,1,0:T(8,128)}, u32[]{:S(2)}, u32[]{:S(2)}) collective-permute-start(f32[2,2,256,128]{3,2,1,0:T(8,128)S(1)} %pad_maximum_fusion), channel_id=1, source_target_pairs={{0,16},{16,32},{32,48},{1,17},{17,33},{33,49},{2,18},{18,34},{34,5... | collective-permute-start | bytes 1572872 | tf_op jit(solution)/shard_map/ppermute | solution.py:391
  26.8 25.3 %copy-start.1 = (f32[2,2,256,128]{3,2,1,0:T(8,128)}, f32[2,2,256,128]{3,2,1,0:T(8,128)S(1)}, u32[]{:S(2)}) copy-start(f32[2,2,256,128]{3,2,1,0:T(8,128)S(1)} %collective-permute-done.2.refs_1_) | copy-start | bytes 1572868
  26.8 25.3 %copy-start.2 = (f32[2,2,256,128]{3,2,1,0:T(8,128)}, f32[2,2,256,128]{3,2,1,0:T(8,128)S(1)}, u32[]{:S(2)}) copy-start(f32[2,2,256,128]{3,2,1,0:T(8,128)S(1)} %collective-permute-done.1.refs_0_) | copy-start | bytes 1572868
  26.8 19.2 %collective-permute-start.7 = (f32[2,2,256,128]{3,2,1,0:T(8,128)}, f32[2,2,256,128]{3,2,1,0:T(8,128)}, u32[]{:S(2)}, u32[]{:S(2)}) collective-permute-start(f32[2,2,256,128]{3,2,1,0:T(8,128)} %collective-permute-done.refs_2_), channel_id=1, source_target_pairs={{0,16},{16,32},{32,48},{1,17},{17,33},{33,49},{2,18},{18,34},{34,5... | collective-permute-start | bytes 1572872 | tf_op jit(solution)/shard_map/ppermute | solution.py:391
  31.8 29.1 %collective-permute-start.6 = (f32[2,2,256,128]{3,2,1,0:T(8,128)}, f32[2,2,256,128]{3,2,1,0:T(8,128)}, u32[]{:S(2)}, u32[]{:S(2)}) collective-permute-start(f32[2,2,256,128]{3,2,1,0:T(8,128)} %collective-permute-done.refs_2_), channel_id=1, source_target_pairs={{0,12},{4,0},{8,4},{12,8},{1,13},{5,1},{9,5},{13,9},{2,14},{6,2},{... | collective-permute-start | bytes 1572872 | tf_op jit(solution)/shard_map/ppermute | solution.py:393
  34.2 35.7 %collective-permute-start.5 = (f32[2,2,256,128]{3,2,1,0:T(8,128)}, f32[2,2,256,128]{3,2,1,0:T(8,128)}, u32[]{:S(2)}, u32[]{:S(2)}) collective-permute-start(f32[2,2,256,128]{3,2,1,0:T(8,128)} %collective-permute-done.refs_2_), channel_id=1, source_target_pairs={{0,4},{4,8},{8,12},{12,0},{1,5},{5,9},{9,13},{13,1},{2,6},{6,10},{... | collective-permute-start | bytes 1572872 | tf_op jit(solution)/shard_map/ppermute | solution.py:392
  35.6 16.5 %copy-start = (f32[1,256,16,128]{3,1,2,0:T(8,128)S(1)}, f32[1,256,16,128]{3,1,2,0:T(8,128)}, u32[]{:S(2)}) copy-start(f32[1,256,16,128]{3,1,2,0:T(8,128)} %copy.35) | copy-start | bytes 6291460
  35.6 16.5 %copy-start.5 = (s32[1,16]{1,0:T(1,128)S(1)}, s32[1,16]{1,0:T(1,128)}, u32[]{:S(2)}) copy-start(s32[1,16]{1,0:T(1,128)} %param.11) | copy-start | bytes 196
  35.6 13.5 %collective-permute-start.4 = (f32[2,256,128]{2,1,0:T(8,128)}, f32[2,256,128]{2,1,0:T(8,128)S(1)}, u32[]{:S(2)}, u32[]{:S(2)}) collective-permute-start(f32[2,256,128]{2,1,0:T(8,128)} %slice_bitcast_fusion.4), channel_id=1, source_target_pairs={{0,12},{4,0},{8,4},{12,8},{1,13},{5,1},{9,5},{13,9},{2,14},{6,2},{... | collective-permute-start | bytes 786440 | tf_op jit(solution)/shard_map/ppermute | solution.py:393
  38.3 13.9 %collective-permute-start.3 = (f32[2,256,128]{2,1,0:T(8,128)}, f32[2,256,128]{2,1,0:T(8,128)}, u32[]{:S(2)}, u32[]{:S(2)}) collective-permute-start(f32[2,256,128]{2,1,0:T(8,128)} %slice_bitcast_fusion.5), channel_id=1, source_target_pairs={{0,4},{4,8},{8,12},{12,0},{1,5},{5,9},{9,13},{13,1},{2,6},{6,10},{... | collective-permute-start | bytes 786440 | tf_op jit(solution)/shard_map/ppermute | solution.py:392
  46.0 162.0 %all-gather.7.cloned.1.call-start = ((), (), s32[]{:S(2)}) async-start(), calls=%async_computation.4 | async-start | bytes 2367488 | tf_op jit(solution)/shard_map/all_gather | solution.py:489
  46.1 24.8 %collective-permute-start.9 = (f32[2,2,256,128]{3,2,1,0:T(8,128)}, f32[2,2,256,128]{3,2,1,0:T(8,128)S(1)}, u32[]{:S(2)}, u32[]{:S(2)}) collective-permute-start(f32[2,2,256,128]{3,2,1,0:T(8,128)} %collective-permute-done.7.refs_2_.refs_5_), channel_id=1, source_target_pairs={{0,12},{4,0},{8,4},{12,8},{1,13},{5,1},{9,5},{13,9},{2,14},{6,2},{... | collective-permute-start | bytes 1572872 | tf_op jit(solution)/shard_map/ppermute | solution.py:393
  49.1 9.5 %copy-start.6 = (f32[2,256,128]{2,1,0:T(8,128)}, f32[2,256,128]{2,1,0:T(8,128)S(1)}, u32[]{:S(2)}) copy-start(f32[2,256,128]{2,1,0:T(8,128)S(1)} %collective-permute-done.4.refs_4_.refs_9_) | copy-start | bytes 786436
  52.2 1.6 copy-start.12
  53.7 1.6 copy-start.13
  58.6 18.3 %collective-permute-start.8 = (f32[2,2,256,128]{3,2,1,0:T(8,128)}, f32[2,2,256,128]{3,2,1,0:T(8,128)S(1)}, u32[]{:S(2)}, u32[]{:S(2)}) collective-permute-start(f32[2,2,256,128]{3,2,1,0:T(8,128)} %collective-permute-done.7.refs_2_.refs_5_), channel_id=1, source_target_pairs={{0,4},{4,8},{8,12},{12,0},{1,5},{5,9},{9,13},{13,1},{2,6},{6,10},{... | collective-permute-start | bytes 1572872 | tf_op jit(solution)/shard_map/ppermute | solution.py:392
  61.8 15.1 %collective-permute-start.11 = (f32[2,256,128]{2,1,0:T(8,128)S(1)}, f32[2,256,128]{2,1,0:T(8,128)S(1)}, u32[]{:S(2)}, u32[]{:S(2)}) collective-permute-start(f32[2,256,128]{2,1,0:T(8,128)S(1)} %slice_bitcast_fusion.2), channel_id=1, source_target_pairs={{0,12},{4,0},{8,4},{12,8},{1,13},{5,1},{9,5},{13,9},{2,14},{6,2},{... | collective-permute-start | bytes 786440 | tf_op jit(solution)/shard_map/ppermute | solution.py:393
  70.8 11.7 %collective-permute-start.10 = (f32[2,256,128]{2,1,0:T(8,128)S(1)}, f32[2,256,128]{2,1,0:T(8,128)S(1)}, u32[]{:S(2)}, u32[]{:S(2)}) collective-permute-start(f32[2,256,128]{2,1,0:T(8,128)S(1)} %slice_bitcast_fusion.3), channel_id=1, source_target_pairs={{0,4},{4,8},{8,12},{12,0},{1,5},{5,9},{9,13},{13,1},{2,6},{6,10},{... | collective-permute-start | bytes 786440 | tf_op jit(solution)/shard_map/ppermute | solution.py:392
  70.9 15.1 %copy-start.3 = (f32[2,2,256,128]{3,2,1,0:T(8,128)}, f32[2,2,256,128]{3,2,1,0:T(8,128)S(1)}, u32[]{:S(2)}) copy-start(f32[2,2,256,128]{3,2,1,0:T(8,128)S(1)} %collective-permute-done.9.refs_4_.refs_7_) | copy-start | bytes 1572868
  70.9 15.2 %collective-permute-start.13 = (f32[2,256,128]{2,1,0:T(8,128)S(1)}, f32[2,256,128]{2,1,0:T(8,128)S(1)}, u32[]{:S(2)}, u32[]{:S(2)}) collective-permute-start(f32[2,256,128]{2,1,0:T(8,128)S(1)} %slice_bitcast_fusion), channel_id=1, source_target_pairs={{0,12},{4,0},{8,4},{12,8},{1,13},{5,1},{9,5},{13,9},{2,14},{6,2},{... | collective-permute-start | bytes 786440 | tf_op jit(solution)/shard_map/ppermute | solution.py:393
  76.8 9.2 %copy-start.4 = (f32[2,2,256,128]{3,2,1,0:T(8,128)}, f32[2,2,256,128]{3,2,1,0:T(8,128)S(1)}, u32[]{:S(2)}) copy-start(f32[2,2,256,128]{3,2,1,0:T(8,128)S(1)} %collective-permute-done.8.refs_3_.refs_6_) | copy-start | bytes 1572868
  76.9 15.4 %collective-permute-start.12 = (f32[2,256,128]{2,1,0:T(8,128)S(1)}, f32[2,256,128]{2,1,0:T(8,128)S(1)}, u32[]{:S(2)}, u32[]{:S(2)}) collective-permute-start(f32[2,256,128]{2,1,0:T(8,128)S(1)} %slice_bitcast_fusion.1), channel_id=1, source_target_pairs={{0,4},{4,8},{8,12},{12,0},{1,5},{5,9},{9,13},{13,1},{2,6},{6,10},{... | collective-permute-start | bytes 786440 | tf_op jit(solution)/shard_map/ppermute | solution.py:392
  77.0 9.1 %copy-start.7 = (f32[2,256,128]{2,1,0:T(8,128)}, f32[2,256,128]{2,1,0:T(8,128)S(1)}, u32[]{:S(2)}) copy-start(f32[2,256,128]{2,1,0:T(8,128)S(1)} %collective-permute-done.11.refs_6_.refs_11_) | copy-start | bytes 786436
  82.5 3.6 %copy-start.8 = (f32[2,256,128]{2,1,0:T(8,128)}, f32[2,256,128]{2,1,0:T(8,128)S(1)}, u32[]{:S(2)}) copy-start(f32[2,256,128]{2,1,0:T(8,128)S(1)} %collective-permute-done.10.refs_5_.refs_10_) | copy-start | bytes 786436
  86.1 9.1 %copy-start.14 = (f32[16,256,128]{2,1,0:T(8,128)}, f32[16,256,128]{2,1,0:T(8,128)S(1)}, u32[]{:S(2)}) copy-start(f32[16,256,128]{2,1,0:T(8,128)S(1)} %get-tuple-element.67.stat_ref) | copy-start | bytes 6291460
  86.1 9.1 %copy-start.9 = (f32[2,256,128]{2,1,0:T(8,128)}, f32[2,256,128]{2,1,0:T(8,128)S(1)}, u32[]{:S(2)}) copy-start(f32[2,256,128]{2,1,0:T(8,128)S(1)} %collective-permute-done.13.refs_1_.refs_13_) | copy-start | bytes 786436
  92.3 2.9 %copy-start.10 = (f32[2,256,128]{2,1,0:T(8,128)}, f32[2,256,128]{2,1,0:T(8,128)S(1)}, u32[]{:S(2)}) copy-start(f32[2,256,128]{2,1,0:T(8,128)S(1)} %collective-permute-done.12.refs_0_.refs_12_) | copy-start | bytes 786436
  95.2 1.3 copy-start.15
  96.5 6.7 %copy-start.11 = (f32[8,256]{1,0:T(8,128)}, f32[8,256]{1,0:T(8,128)S(1)}, u32[]{:S(2)}) copy-start(f32[8,256]{1,0:T(8,128)S(1)} %get-tuple-element.73.sq0_ref) | copy-start | bytes 24580
  96.5 3.7 %collective-permute-start.16 = (f32[8,256]{1,0:T(8,128)S(1)}, f32[8,256]{1,0:T(8,128)S(1)}, u32[]{:S(2)}, u32[]{:S(2)}) collective-permute-start(f32[8,256]{1,0:T(8,128)S(1)} %get-tuple-element.73.sq0_ref), channel_id=1, source_target_pairs={{0,3},{1,0},{2,1},{3,2},{4,7},{5,4},{6,5},{7,6},{8,11},{9,8},{10,9... | collective-permute-start | bytes 24584 | tf_op jit(solution)/shard_map/ppermute | solution.py:462
  99.1 4.0 %collective-permute-start.15 = (f32[8,256]{1,0:T(8,128)S(1)}, f32[8,256]{1,0:T(8,128)S(1)}, u32[]{:S(2)}, u32[]{:S(2)}) collective-permute-start(f32[8,256]{1,0:T(8,128)S(1)} %get-tuple-element.73.sq0_ref), channel_id=1, source_target_pairs={{0,2},{1,3},{2,0},{3,1},{4,6},{5,7},{6,4},{7,5},{8,10},{9,11},{10,... | collective-permute-start | bytes 24584 | tf_op jit(solution)/shard_map/ppermute | solution.py:462
  99.5 3.7 %collective-permute-start.14 = (f32[8,256]{1,0:T(8,128)S(1)}, f32[8,256]{1,0:T(8,128)S(1)}, u32[]{:S(2)}, u32[]{:S(2)}) collective-permute-start(f32[8,256]{1,0:T(8,128)S(1)} %get-tuple-element.73.sq0_ref), channel_id=1, source_target_pairs={{0,1},{1,2},{2,3},{3,0},{4,5},{5,6},{6,7},{7,4},{8,9},{9,10},{10,1... | collective-permute-start | bytes 24584 | tf_op jit(solution)/shard_map/ppermute | solution.py:462
  100.2 3.1 %copy-start.18 = (f32[8,256]{1,0:T(8,128)}, f32[8,256]{1,0:T(8,128)S(1)}, u32[]{:S(2)}) copy-start(f32[8,256]{1,0:T(8,128)S(1)} %collective-permute-done.16.sq3_ref) | copy-start | bytes 24580
  103.1 0.6 copy-start.19
  103.3 0.6 copy-start.20
  120.3 48.9 %all-to-all-start = ((f32[32,64,128]{2,1,0:T(8,128)}), f32[32,64,128]{2,1,0:T(8,128)S(1)}, u32[]{:S(2)}, u32[]{:S(2)}) async-start(f32[32,64,128]{2,1,0:T(8,128)} %bitcast.61), calls=%async_computation | async-start | bytes 2097152 | tf_op jit(solution)/shard_map/all_to_all | solution.py:490
  169.3 19.0 %copy-start.17 = (f32[16,256,128]{2,1,0:T(8,128)S(1)}, f32[16,256,128]{2,1,0:T(8,128)}, u32[]{:S(2)}) copy-start(f32[16,256,128]{2,1,0:T(8,128)} %get-tuple-element.74) | copy-start | bytes 6291460
  183.8 22.4 %all-to-all-start.2 = ((f32[32,72,128]{2,1,0:T(8,128)}), f32[32,72,128]{2,1,0:T(8,128)S(1)}, u32[]{:S(2)}, u32[]{:S(2)}) async-start(f32[32,72,128]{2,1,0:T(8,128)} %broadcast_in_dim.15), calls=%async_computation.2 | async-start | bytes 2359296 | tf_op jit(solution)/shard_map/all_to_all | solution.py:509
Sparse Core Ops, SparseCore 0:
  46.1 53.5 all-gather.4
  120.4 70.4 all-gather.6
